TPU v7x, 128 devices: a whole 4x4x4 slice. The times are simulated.
128 devices in a mesh: slide: 32 (over y_lo, x, z), region: 4 (over y_hi, core).
Axes of the slice: x: 4, y: 4 (y_hi: 2, y_lo: 2; y = y_hi * 2 + y_lo), z: 4, core: 2. Of those that a mesh axis runs over, the one named last changes fastest.
Arguments:
- tiles: bfloat16 [32, 4, 32, 196, 1024], P('slide', 'region'), may hold values from -6 to 6
- counts: int32 [32, 4], P('slide', 'region'), may hold values from 1 to 31, as said below
- tissue_mask: int32 [32, 4, 32, 196], P('slide', 'region'), may hold values 0 or 1
- w_reduce: bfloat16 [2, 1024, 256], replicated, may hold values from -0.1875 to 0.1875
- b_reduce: float32 [2, 256], replicated, may hold values from -3 to 3
- w_spatial: bfloat16 [2, 9, 256, 256], replicated, may hold values from -0.125 to 0.125
- b_spatial: float32 [2, 256], replicated, may hold values from -3 to 3
- w_expand: bfloat16 [2, 256, 1024], replicated, may hold values from -0.375 to 0.375
- proj_w: bfloat16 [1024, 256], replicated, may hold values from -0.1875 to 0.1875
Outputs:
- embedded: float32 [32, 4, 32, 196, 256], P('slide', 'region')
Inputs may be any that keep to these rules, and one draw needn't show every extreme that they name: For each region, the counts of slide s and slide s + 16 add up to at most 32.
All inputs are finite; a program needn't handle non-finite values. No bound on the sum of `tissue_mask` on one device may be relied on, other than what follows from the above.
Results may differ from a plain program's by a relative error of at most 0.0022.
Values may be sent and summed in bfloat16 or wider, within the bound.
A program may use at most 192 MiB of HBM per device.

v0:
```python
import jax
import jax.numpy as jnp
from jax import lax
from jax.experimental import pallas as pl
from jax.experimental.pallas import tpu as pltpu
from jax.sharding import PartitionSpec as P

CHAN = 1024
MID = 256
TILE = 14
BLOCKS = 2
TCOLS = 4
CELLS = TILE * TILE
WIDE = 16
PADDED = TILE * WIDE


def tile_kernel(
    count_ref, x_ref, m_ref, wr_ref, br_ref, ws_ref, bs_ref, we_ref, pw_ref, o_ref,
    cur_ref, r_ref, s_ref, c_ref, q_ref,
):
    t = pl.program_id(0)

    @pl.when(t >= count_ref[0])
    def _():
        o_ref[...] = jnp.zeros(o_ref.shape, o_ref.dtype)

    @pl.when(t < count_ref[0])
    def _():
        s_ref[...] = jnp.zeros(s_ref.shape, s_ref.dtype)
        c_ref[0:WIDE, :] = jnp.zeros((WIDE, 3 * MID), jnp.bfloat16)
        c_ref[WIDE + PADDED:, :] = jnp.zeros((WIDE, 3 * MID), jnp.bfloat16)
        cur_ref[...] = x_ref[0]
        for b in range(BLOCKS):
            x = cur_ref[...]
            r = jnp.dot(x, wr_ref[b], preferred_element_type=jnp.float32) + br_ref[b]
            r_ref[...] = jnp.maximum(r, 0.0)
            for i in range(TILE):
                s_ref[pl.ds(8 + WIDE * i, TILE), :] = r_ref[pl.ds(TILE * i, TILE), :]
            c_ref[WIDE : WIDE + PADDED, 0:MID] = s_ref[pl.ds(7, PADDED), :].astype(jnp.bfloat16)
            c_ref[WIDE : WIDE + PADDED, MID : 2 * MID] = s_ref[pl.ds(8, PADDED), :].astype(jnp.bfloat16)
            c_ref[WIDE : WIDE + PADDED, 2 * MID :] = s_ref[pl.ds(9, PADDED), :].astype(jnp.bfloat16)
            acc = jnp.dot(c_ref[0:PADDED, :], ws_ref[b, 0], preferred_element_type=jnp.float32)
            acc += jnp.dot(c_ref[WIDE : WIDE + PADDED, :], ws_ref[b, 1], preferred_element_type=jnp.float32)
            acc += jnp.dot(c_ref[2 * WIDE : 2 * WIDE + PADDED, :], ws_ref[b, 2], preferred_element_type=jnp.float32)
            q_ref[...] = jnp.maximum(acc + bs_ref[b], 0.0)
            for i in range(TILE):
                r_ref[pl.ds(TILE * i, TILE), :] = q_ref[pl.ds(WIDE * i, TILE), :]
            spatial = r_ref[...].astype(jnp.bfloat16)
            e = jnp.dot(spatial, we_ref[b], preferred_element_type=jnp.float32)
            cur_ref[...] = jnp.maximum(x.astype(jnp.float32) + e, 0.0).astype(jnp.bfloat16)
        proj = jnp.dot(cur_ref[...], pw_ref[...], preferred_element_type=jnp.float32)
        o_ref[0] = proj * m_ref[0]


def tile_features(count, x, weight, w_reduce, b_reduce, w_spatial, b_spatial, w_expand, proj_w):
    slots = x.shape[0]
    emb = proj_w.shape[1]
    ws = w_spatial.reshape(BLOCKS, 3, 3 * MID, MID)
    br = b_reduce.reshape(BLOCKS, 1, MID)
    bs = b_spatial.reshape(BLOCKS, 1, MID)

    def live(t, c):
        return (jnp.maximum(jnp.minimum(t, c[0] - 1), 0), 0, 0)

    def whole(nd):
        return lambda t, c: (0,) * nd

    grid_spec = pltpu.PrefetchScalarGridSpec(
        num_scalar_prefetch=1,
        grid=(slots,),
        in_specs=[
            pl.BlockSpec((1, CELLS, CHAN), live),
            pl.BlockSpec((1, CELLS, 1), lambda t, c: (t, 0, 0)),
            pl.BlockSpec((BLOCKS, CHAN, MID), whole(3)),
            pl.BlockSpec((BLOCKS, 1, MID), whole(3)),
            pl.BlockSpec((BLOCKS, 3, 3 * MID, MID), whole(4)),
            pl.BlockSpec((BLOCKS, 1, MID), whole(3)),
            pl.BlockSpec((BLOCKS, MID, CHAN), whole(3)),
            pl.BlockSpec((CHAN, emb), whole(2)),
        ],
        out_specs=pl.BlockSpec((1, CELLS, emb), lambda t, c: (t, 0, 0)),
        scratch_shapes=[
            pltpu.VMEM((CELLS, CHAN), jnp.bfloat16),
            pltpu.VMEM((CELLS, MID), jnp.float32),
            pltpu.VMEM((PADDED + WIDE, MID), jnp.float32),
            pltpu.VMEM((PADDED + 2 * WIDE, 3 * MID), jnp.bfloat16),
            pltpu.VMEM((PADDED, MID), jnp.float32),
        ],
    )
    flops = 2 * slots * CELLS * (BLOCKS * (2 * CHAN * MID + 9 * MID * MID) + CHAN * emb)
    return pl.pallas_call(
        tile_kernel,
        grid_spec=grid_spec,
        out_shape=jax.ShapeDtypeStruct((slots, CELLS, emb), jnp.float32),
        compiler_params=pltpu.CompilerParams(
            dimension_semantics=("arbitrary",), vmem_limit_bytes=48 * 1024 * 1024
        ),
        cost_estimate=pl.CostEstimate(
            flops=flops, transcendentals=0, bytes_accessed=slots * CELLS * (2 * CHAN + 4 * emb + 4)
        ),
    )(count, x, weight, w_reduce, br, ws, bs, w_expand, proj_w)


def with_halo(block, sides, width):
    for axis, dim in sides:
        count = lax.axis_size(axis)
        forward = [(i, i + 1) for i in range(count - 1)]
        backward = [(target, source) for source, target in forward]
        low = lax.ppermute(
            lax.slice_in_dim(block, block.shape[dim] - width, None, axis=dim), axis, forward
        )
        high = lax.ppermute(lax.slice_in_dim(block, 0, width, axis=dim), axis, backward)
        block = jnp.concatenate([low, block, high], axis=dim)
    return block


def per_device(
    tiles, counts, tissue_mask, w_reduce, b_reduce, w_spatial, b_spatial, w_expand, proj_w
):
    slots = tiles.shape[2]
    held = counts[0]
    positions = jnp.arange(slots, dtype=jnp.int32)
    alive = positions < held[0]
    weight = jnp.where(alive[:, None], tissue_mask[0, 0], 0).astype(jnp.float32)
    weighted = tile_features(
        held, tiles[0, 0], weight[:, :, None], w_reduce, b_reduce, w_spatial, b_spatial, w_expand, proj_w
    )
    tile_rows = slots // TCOLS
    image = weighted.reshape(tile_rows, TCOLS, TILE, TILE, -1).transpose(0, 2, 1, 3, 4)
    image = image.reshape(tile_rows * TILE, TCOLS * TILE, -1)
    height = image.shape[0]
    width = image.shape[1]
    extended = with_halo(image, (("region", 0),), 1)
    framed = jnp.pad(extended, ((0, 0), (1, 1), (0, 0)))
    total = jnp.zeros_like(image)
    for row_off in range(3):
        for col_off in range(3):
            total = total + framed[row_off : row_off + height, col_off : col_off + width, :]
    averaged = total / 9.0
    averaged = averaged.reshape(tile_rows, TILE, TCOLS, TILE, -1).transpose(0, 2, 1, 3, 4)
    return averaged.reshape(1, 1, slots, TILE * TILE, -1)


def solution(mesh):
    placed = (
        P("slide", "region", None, None, None),
        P("slide", "region"),
        P("slide", "region", None, None),
        P(),
        P(),
        P(),
        P(),
        P(),
        P(),
    )
    return jax.shard_map(
        per_device,
        mesh=mesh,
        in_specs=placed,
        out_specs=P("slide", "region", None, None, None),
        check_vma=False,
    )
```

profile of v0, /device:TPU:5, one launch (start us, length us, event | category | flops | bytes accessed | tf_op | source)
XLA Modules:
  0.0 191.2 jit_solution(17261449793928983993)
XLA Ops:
  0.7 0.7 reshape.59.br_ref
  1.4 0.7 reshape.61.bs_ref
  2.0 1.8 copy.16
  3.9 11.2 %copy.23 = bf16[1,1,32,196,1024]{4,3,2,1,0:T(8,128)(2,1)} copy(bf16[1,1,32,196,1024]{4,2,3,1,0:T(8,128)(2,1)} %param.9) | data formatting | bytes 25690112 | tf_op args[0]
  15.1 0.0 copy-start
  15.1 0.0 copy-start.1
  15.1 0.0 copy-start.2
  15.1 0.0 copy-start.3
  15.1 2.1 %select_convert_fusion.m_ref = f32[32,196,1]{2,1,0:T(8,128)} fusion(s32[32,196,1]{2,1,0:T(8,128)S(1)} %copy.16, pred[32]{0:T(512)(128)(4,1)S(1)} %iota_compare_fusion.2), kind=kLoop, calls=%fused_computation.18 | loop fusion | flops 12544 | bytes 50208 | tf_op jit(solution)/shard_map/convert_element_type | solution.py:125
  17.2 0.3 copy-done
  17.5 0.7 copy-done.1
  18.2 0.3 copy-done.2
  18.5 0.1 copy-done.3
  18.6 27.6 %shard_map.91 = f32[32,196,256]{2,1,0:T(8,128)} custom-call(s32[1]{0:T(128)} %bitcast.13.count_ref, bf16[32,196,1024]{2,1,0:T(8,128)(2,1)} %bitcast.18, f32[32,196,1]{2,1,0:T(8,128)} %select_convert_fusion.m_ref, bf16[2,1024,256]{2,1,0:T(8,128)(2,1)S(1)} %copy-done.1, f32[2,1,256]{2,1,0:T(1,128)S(1)} %reshape.59.br_ref, ...), custom_call_target="tpu_custom_call" | custom-call | flops 31239176192 | bytes 19292672 | tf_op jit(solution)/shard_map/pallas_call | solution.py:92
  46.3 7.9 %reshape.66 = f32[8,4,14,14,256]{4,3,2,1,0:T(8,128)} reshape(f32[32,196,256]{2,1,0:T(8,128)} %shard_map.91) | data formatting | bytes 12845056 | tf_op jit(solution)/shard_map/reshape | solution.py:130
  54.2 7.2 %copy.24 = f32[8,4,14,14,256]{4,1,0,3,2:T(4,128)S(1)} copy(f32[8,4,14,14,256]{4,3,2,1,0:T(8,128)} %reshape.66) | data formatting | bytes 12845056 | tf_op jit(solution)/shard_map/reshape | solution.py:130
  61.4 6.7 %copy.18 = f32[8,14,4,14,256]{4,3,2,1,0:T(8,128)} copy(f32[8,14,4,14,256]{4,2,0,3,1:T(4,128)S(1)} %bitcast.17) | data formatting | bytes 12845056 | tf_op jit(solution)/shard_map/transpose | solution.py:130
  68.1 7.7 %reshape.63 = f32[112,56,256]{2,1,0:T(8,128)} reshape(f32[8,14,4,14,256]{4,3,2,1,0:T(8,128)} %copy.18) | data formatting | bytes 12845056 | tf_op jit(solution)/shard_map/reshape | solution.py:131
  75.9 0.9 fusion.5
  76.7 64.8 %collective-permute-start = (f32[1,56,256]{2,1,0:T(8,128)S(1)}, f32[1,56,256]{2,1,0:T(8,128)S(1)}, u32[]{:S(2)}, u32[]{:S(2)}) collective-permute-start(f32[1,56,256]{2,1,0:T(8,128)S(1)} %get-tuple-element.5), channel_id=1, source_target_pairs={{0,1},{1,2},{2,3},{4,5},{5,6},{6,7},{8,9},{9,10},{10,11},{12,13},{... | collective-permute-start | bytes 172040 | tf_op jit(solution)/shard_map/ppermute | solution.py:110
  141.6 1.9 %collective-permute-start.1 = (f32[1,56,256]{2,1,0:T(8,128)S(1)}, f32[1,56,256]{2,1,0:T(8,128)S(1)}, u32[]{:S(2)}, u32[]{:S(2)}) collective-permute-start(f32[1,56,256]{2,1,0:T(8,128)S(1)} %get-tuple-element.6), channel_id=1, source_target_pairs={{1,0},{2,1},{3,2},{5,4},{6,5},{7,6},{9,8},{10,9},{11,10},{13,12},{... | collective-permute-start | bytes 172040 | tf_op jit(solution)/shard_map/ppermute | solution.py:113
  143.5 0.0 collective-permute-done
  143.5 5.1 %collective-permute-done.1 = f32[1,56,256]{2,1,0:T(8,128)S(1)} collective-permute-done((f32[1,56,256]{2,1,0:T(8,128)S(1)}, f32[1,56,256]{2,1,0:T(8,128)S(1)}, u32[]{:S(2)}, u32[]{:S(2)}) %collective-permute-start.1) | collective-permute-done | bytes 57376 | tf_op jit(solution)/shard_map/ppermute | solution.py:113
  148.6 3.6 %select_maximum_fusion = f32[114,58,256]{2,1,0:T(8,128)S(1)} fusion(f32[1,56,256]{2,1,0:T(8,128)S(1)} %collective-permute-done.1, f32[112,56,256]{2,1,0:T(8,128)} %reshape.63, f32[1,56,256]{2,1,0:T(8,128)S(1)} %collective-permute-done), kind=kLoop, calls=%fused_computation.3 | loop fusion | flops 13541376 | bytes 13307904 | tf_op jit(solution)/shard_map/concatenate | solution.py:114
  152.1 13.3 %fusion.1 = f32[112,56,256]{2,1,0:T(8,128)} fusion(f32[114,58,256]{2,1,0:T(8,128)S(1)} %select_maximum_fusion, f32[1,56,256]{2,1,0:T(8,128)S(1)} %collective-permute-done.1, f32[112,56,256]{2,1,0:T(8,128)} %reshape.63, f32[1,56,256]{2,1,0:T(8,128)S(1)} %collective-permute-done), kind=kLoop, calls=%fused_computation.7 | loop fusion | flops 17661952 | bytes 51494912 | tf_op jit(solution)/shard_map/div | solution.py:140
  165.5 7.7 %reshape.64 = f32[8,14,4,14,256]{4,3,2,1,0:T(8,128)} reshape(f32[112,56,256]{2,1,0:T(8,128)} %fusion.1) | data formatting | bytes 12845056 | tf_op jit(solution)/shard_map/reshape | solution.py:141
  173.1 10.0 %copy.19 = f32[8,4,14,14,256]{4,1,0,3,2:T(4,128)} copy(f32[8,4,14,14,256]{4,3,1,2,0:T(8,128)} %bitcast.16) | data formatting | bytes 12845056 | tf_op jit(solution)/shard_map/transpose | solution.py:141
  183.1 8.1 %reshape.65 = f32[1,1,32,196,256]{4,2,3,1,0:T(8,128)} reshape(f32[8,4,14,14,256]{4,1,0,3,2:T(4,128)} %copy.19) | data formatting | bytes 12845056 | tf_op jit(solution)/shard_map/reshape | solution.py:142
  (1 shorter events, 0.0 us)
Async XLA Ops:
  15.1 2.4 %copy-start = (bf16[2,9,256,256]{3,2,1,0:T(8,128)(2,1)S(1)}, bf16[2,9,256,256]{3,2,1,0:T(8,128)(2,1)}, u32[]{:S(2)}) copy-start(bf16[2,9,256,256]{3,2,1,0:T(8,128)(2,1)} %param.14) | copy-start | bytes 7077892
  15.1 3.1 %copy-start.1 = (bf16[2,1024,256]{2,1,0:T(8,128)(2,1)S(1)}, bf16[2,1024,256]{2,1,0:T(8,128)(2,1)}, u32[]{:S(2)}) copy-start(bf16[2,1024,256]{2,1,0:T(8,128)(2,1)} %wr_ref.1) | copy-start | bytes 3145732
  15.1 3.4 %copy-start.2 = (bf16[2,256,1024]{2,1,0:T(8,128)(2,1)S(1)}, bf16[2,256,1024]{2,1,0:T(8,128)(2,1)}, u32[]{:S(2)}) copy-start(bf16[2,256,1024]{2,1,0:T(8,128)(2,1)} %we_ref.1) | copy-start | bytes 3145732
  15.1 3.6 %copy-start.3 = (bf16[1024,256]{1,0:T(8,128)(2,1)S(1)}, bf16[1024,256]{1,0:T(8,128)(2,1)}, u32[]{:S(2)}) copy-start(bf16[1024,256]{1,0:T(8,128)(2,1)} %pw_ref.1) | copy-start | bytes 1572868
  76.7 66.8 %collective-permute-start = (f32[1,56,256]{2,1,0:T(8,128)S(1)}, f32[1,56,256]{2,1,0:T(8,128)S(1)}, u32[]{:S(2)}, u32[]{:S(2)}) collective-permute-start(f32[1,56,256]{2,1,0:T(8,128)S(1)} %get-tuple-element.5), channel_id=1, source_target_pairs={{0,1},{1,2},{2,3},{4,5},{5,6},{6,7},{8,9},{9,10},{10,11},{12,13},{... | collective-permute-start | bytes 172040 | tf_op jit(solution)/shard_map/ppermute | solution.py:110
  141.6 7.0 %collective-permute-start.1 = (f32[1,56,256]{2,1,0:T(8,128)S(1)}, f32[1,56,256]{2,1,0:T(8,128)S(1)}, u32[]{:S(2)}, u32[]{:S(2)}) collective-permute-start(f32[1,56,256]{2,1,0:T(8,128)S(1)} %get-tuple-element.6), channel_id=1, source_target_pairs={{1,0},{2,1},{3,2},{5,4},{6,5},{7,6},{9,8},{10,9},{11,10},{13,12},{... | collective-permute-start | bytes 172040 | tf_op jit(solution)/shard_map/ppermute | solution.py:113
where the time goes:
time: 193 us; the launch traced here: 191 us
  local copies, waits for them, and re-layouts  72 us (37%)
  starting transfers between devices  66.8 us (35%)
  Pallas kernels  27.6 us (14%)
  other arithmetic  19 us (10%)
  waiting for transfers between devices  5.06 us (3%)
    ppermute x1, starting transfers between devices, with_halo(): lax.ppermute(lax.slice_in_dim(block, block.shape[dim] - width, None, axis...  64.8 us
    pallas_call x1, Pallas kernels, tile_features(): pl.pallas_call(tile_kernel, grid_spec=grid_spec, out_shape=jax.ShapeDtype...  27.6 us
    reshape x2, local copies, waits for them, and re-layouts, per_device(): weighted.reshape(tile_rows, TCOLS, TILE, TILE, -1).transpose(0, 2, 1, 3, 4)  15.1 us
    div x1, other arithmetic, per_device(): averaged = total / 9.0  13.3 us
    unnamed x9, local copies, waits for them, and re-layouts  12.7 us
    transpose x1, local copies, waits for them, and re-layouts, per_device(): averaged.reshape(tile_rows, TILE, TCOLS, TILE, -1).transpose(0, 2, 1, 3, 4)  9.99 us
    reshape x1, local copies, waits for them, and re-layouts, per_device(): return averaged.reshape(1, 1, slots, TILE * TILE, -1)  8.09 us
    reshape x1, local copies, waits for them, and re-layouts, per_device(): image = image.reshape(tile_rows * TILE, TCOLS * TILE, -1)  7.74 us
  transfers between devices with their start and end apart: 2, of which 1 were waited for; matrix products, arithmetic and copies ran while one was open for 0% of the time, Pallas kernels for 0%

commit v1 on v0

--- a/solution.py
+++ b/solution.py
@@ -102,17 +102,74 @@
     )(count, x, weight, w_reduce, br, ws, bs, w_expand, proj_w)
 
 
-def with_halo(block, sides, width):
-    for axis, dim in sides:
-        count = lax.axis_size(axis)
-        forward = [(i, i + 1) for i in range(count - 1)]
-        backward = [(target, source) for source, target in forward]
-        low = lax.ppermute(
-            lax.slice_in_dim(block, block.shape[dim] - width, None, axis=dim), axis, forward
-        )
-        high = lax.ppermute(lax.slice_in_dim(block, 0, width, axis=dim), axis, backward)
-        block = jnp.concatenate([low, block, high], axis=dim)
-    return block
+GUARD = 16
+
+
+def box_kernel(w_ref, hu_ref, hd_ref, j_ref, o_ref, g_ref, v_ref):
+    tr = pl.program_id(0)
+    rows = pl.num_programs(0)
+    col = j_ref[...]
+    for tc in range(TCOLS):
+        t = tr * TCOLS + tc
+        g_ref[TILE : TILE + CELLS, :] = w_ref[t]
+
+        @pl.when(tr == 0)
+        def _():
+            g_ref[0:TILE, :] = hu_ref[tc]
+
+        @pl.when(tr > 0)
+        def _():
+            g_ref[0:TILE, :] = w_ref[t - TCOLS, CELLS - TILE : CELLS, :]
+
+        @pl.when(tr == rows - 1)
+        def _():
+            g_ref[TILE + CELLS : 2 * TILE + CELLS, :] = hd_ref[tc]
+
+        @pl.when(tr < rows - 1)
+        def _():
+            g_ref[TILE + CELLS : 2 * TILE + CELLS, :] = w_ref[t + TCOLS, 0:TILE, :]
+
+        v = g_ref[0:CELLS, :] + g_ref[TILE : TILE + CELLS, :] + g_ref[2 * TILE : 2 * TILE + CELLS, :]
+        v_ref[tc, GUARD : GUARD + CELLS, :] = v
+    for tc in range(TCOLS):
+        h = v_ref[tc, GUARD : GUARD + CELLS, :]
+        h = h + jnp.where(col != 0, v_ref[tc, GUARD - 1 : GUARD - 1 + CELLS, :], 0.0)
+        h = h + jnp.where(col != TILE - 1, v_ref[tc, GUARD + 1 : GUARD + 1 + CELLS, :], 0.0)
+        if tc > 0:
+            h = h + jnp.where(col == 0, v_ref[tc - 1, GUARD + TILE - 1 : GUARD + TILE - 1 + CELLS, :], 0.0)
+        if tc < TCOLS - 1:
+            h = h + jnp.where(
+                col == TILE - 1, v_ref[tc + 1, GUARD - TILE + 1 : GUARD - TILE + 1 + CELLS, :], 0.0
+            )
+        o_ref[tc] = h / 9.0
+
+
+def box_average(w, up, down):
+    slots, cells, emb = w.shape
+    rows = slots // TCOLS
+    col = jnp.broadcast_to((jnp.arange(cells, dtype=jnp.int32) % TILE)[:, None], (cells, emb))
+    return pl.pallas_call(
+        box_kernel,
+        grid=(rows,),
+        in_specs=[
+            pl.BlockSpec((slots, cells, emb), lambda r: (0, 0, 0)),
+            pl.BlockSpec((TCOLS, TILE, emb), lambda r: (0, 0, 0)),
+            pl.BlockSpec((TCOLS, TILE, emb), lambda r: (0, 0, 0)),
+            pl.BlockSpec((cells, emb), lambda r: (0, 0)),
+        ],
+        out_specs=pl.BlockSpec((TCOLS, cells, emb), lambda r: (r, 0, 0)),
+        out_shape=jax.ShapeDtypeStruct(w.shape, jnp.float32),
+        scratch_shapes=[
+            pltpu.VMEM((2 * TILE + CELLS, emb), jnp.float32),
+            pltpu.VMEM((TCOLS, 2 * GUARD + CELLS, emb), jnp.float32),
+        ],
+        compiler_params=pltpu.CompilerParams(
+            dimension_semantics=("arbitrary",), vmem_limit_bytes=48 * 1024 * 1024
+        ),
+        cost_estimate=pl.CostEstimate(
+            flops=10 * slots * cells * emb, transcendentals=0, bytes_accessed=8 * slots * cells * emb
+        ),
+    )(w, up, down, col)
 
 
 def per_device(
@@ -126,20 +183,13 @@
     weighted = tile_features(
         held, tiles[0, 0], weight[:, :, None], w_reduce, b_reduce, w_spatial, b_spatial, w_expand, proj_w
     )
-    tile_rows = slots // TCOLS
-    image = weighted.reshape(tile_rows, TCOLS, TILE, TILE, -1).transpose(0, 2, 1, 3, 4)
-    image = image.reshape(tile_rows * TILE, TCOLS * TILE, -1)
-    height = image.shape[0]
-    width = image.shape[1]
-    extended = with_halo(image, (("region", 0),), 1)
-    framed = jnp.pad(extended, ((0, 0), (1, 1), (0, 0)))
-    total = jnp.zeros_like(image)
-    for row_off in range(3):
-        for col_off in range(3):
-            total = total + framed[row_off : row_off + height, col_off : col_off + width, :]
-    averaged = total / 9.0
-    averaged = averaged.reshape(tile_rows, TILE, TCOLS, TILE, -1).transpose(0, 2, 1, 3, 4)
-    return averaged.reshape(1, 1, slots, TILE * TILE, -1)
+    count = lax.axis_size("region")
+    forward = [(i, i + 1) for i in range(count - 1)]
+    backward = [(target, source) for source, target in forward]
+    up = lax.ppermute(weighted[slots - TCOLS :, CELLS - TILE :], "region", forward)
+    down = lax.ppermute(weighted[:TCOLS, :TILE], "region", backward)
+    averaged = box_average(weighted, up, down)
+    return averaged.reshape(1, 1, slots, CELLS, -1)
 
 
 def solution(mesh):

time: 193 us -> 136 us (0.70)
  the two profiles are of different devices: /device:TPU:5 before, /device:TPU:15 now
where the time goes in v1:
time: 136 us; the launch traced here: 135 us
  Pallas kernels  99.8 us (73%)
  local copies, waits for them, and re-layouts  23.2 us (17%)
  waiting for transfers between devices  4.65 us (3%)
  starting transfers between devices  4.33 us (3%)
  other arithmetic  2.09 us (2%)
    pallas_call x1, Pallas kernels, tile_features(): pl.pallas_call(tile_kernel, grid_spec=grid_spec, out_shape=jax.ShapeDtype...  88.2 us
    unnamed x13, local copies, waits for them, and re-layouts  12.7 us
    pallas_call x1, Pallas kernels, box_average(): pl.pallas_call(box_kernel, grid=(rows,), in_specs=[pl.BlockSpec((slots, c...  11.6 us
    reshape x1, local copies, waits for them, and re-layouts, per_device(): return averaged.reshape(1, 1, slots, CELLS, -1)  7.67 us
    ppermute x1, waiting for transfers between devices, per_device(): down = lax.ppermute(weighted[:TCOLS, :TILE], 'region', backward)  4.65 us
  transfers between devices with their start and end apart: 2, of which 1 were waited for; matrix products, arithmetic and copies ran while one was open for 0% of the time, Pallas kernels for 0%

profile of v1, /device:TPU:15, one launch (start us, length us, event | category | flops | bytes accessed | tf_op | source)
XLA Modules:
  0.0 134.9 jit_solution(14299943757371532341)
XLA Ops:
  0.7 1.8 %copy.13 = s32[32,196,1]{2,1,0:T(8,128)S(1)} copy(s32[32,196,1]{1,0,2:T(8,128)} %bitcast.13) | data formatting | bytes 50176 | tf_op jit(solution)/shard_map/squeeze | solution.py:182
  2.5 0.0 copy-start.4
  2.5 0.0 copy-start.5
  2.5 11.2 %copy.16 = bf16[1,1,32,196,1024]{4,3,2,1,0:T(8,128)(2,1)} copy(bf16[1,1,32,196,1024]{4,2,3,1,0:T(8,128)(2,1)} %param.9) | data formatting | bytes 25690112 | tf_op args[0]
  13.7 0.0 copy-done.4
  13.7 0.0 copy-done.5
  13.8 0.0 copy-start
  13.8 0.0 copy-start.1
  13.8 0.0 copy-start.2
  13.8 0.0 copy-start.3
  13.8 2.1 %select_convert_fusion.m_ref = f32[32,196,1]{2,1,0:T(8,128)} fusion(s32[32,196,1]{2,1,0:T(8,128)S(1)} %copy.13, pred[32]{0:T(512)(128)(4,1)S(1)} %iota_compare_fusion), kind=kLoop, calls=%fused_computation.1 | loop fusion | flops 12544 | bytes 50208 | tf_op jit(solution)/shard_map/convert_element_type | solution.py:182
  15.9 0.3 copy-done
  16.1 0.7 copy-done.1
  16.9 0.3 copy-done.2
  17.2 0.1 copy-done.3
  17.3 88.2 %shard_map.91.w_ref = f32[32,196,256]{2,1,0:T(8,128)} custom-call(s32[1]{0:T(128)} %bitcast.8.count_ref, bf16[32,196,1024]{2,1,0:T(8,128)(2,1)} %bitcast.12, f32[32,196,1]{2,1,0:T(8,128)} %select_convert_fusion.m_ref, bf16[2,1024,256]{2,1,0:T(8,128)(2,1)S(1)} %copy-done.1, f32[2,1,256]{2,1,0:T(1,128)S(1)} %reshape.59.br_ref, ...), custom_call_target="tpu_custom_call" | custom-call | flops 31239176192 | bytes 19292672 | tf_op jit(solution)/shard_map/pallas_call | solution.py:92
  105.6 0.9 fusion
  106.5 1.9 %collective-permute-start = (f32[4,14,256]{2,1,0:T(8,128)S(1)}, f32[4,14,256]{2,1,0:T(8,128)S(1)}, u32[]{:S(2)}, u32[]{:S(2)}) collective-permute-start(f32[4,14,256]{2,1,0:T(8,128)S(1)} %get-tuple-element.6), channel_id=1, source_target_pairs={{0,1},{1,2},{2,3},{4,5},{5,6},{6,7},{8,9},{9,10},{10,11},{12,13},{... | collective-permute-start | bytes 172040 | tf_op jit(solution)/shard_map/ppermute | solution.py:189
  108.5 2.4 %collective-permute-start.1 = (f32[4,14,256]{2,1,0:T(8,128)S(1)}, f32[4,14,256]{2,1,0:T(8,128)S(1)}, u32[]{:S(2)}, u32[]{:S(2)}) collective-permute-start(f32[4,14,256]{2,1,0:T(8,128)S(1)} %get-tuple-element.5), channel_id=1, source_target_pairs={{1,0},{2,1},{3,2},{5,4},{6,5},{7,6},{9,8},{10,9},{11,10},{13,12},{... | collective-permute-start | bytes 172040 | tf_op jit(solution)/shard_map/ppermute | solution.py:190
  110.9 0.0 collective-permute-done.hu_ref
  110.9 4.7 %collective-permute-done.1.hd_ref = f32[4,14,256]{2,1,0:T(8,128)S(1)} collective-permute-done((f32[4,14,256]{2,1,0:T(8,128)S(1)}, f32[4,14,256]{2,1,0:T(8,128)S(1)}, u32[]{:S(2)}, u32[]{:S(2)}) %collective-permute-start.1) | collective-permute-done | bytes 57376 | tf_op jit(solution)/shard_map/ppermute | solution.py:190
  115.5 0.1 broadcast_in_dim.22.j_ref
  115.6 11.6 %shard_map.92 = f32[32,196,256]{2,1,0:T(8,128)} custom-call(f32[32,196,256]{2,1,0:T(8,128)} %shard_map.91.w_ref, f32[4,14,256]{2,1,0:T(8,128)S(1)} %collective-permute-done.hu_ref, f32[4,14,256]{2,1,0:T(8,128)S(1)} %collective-permute-done.1.hd_ref, s32[196,256]{1,0:T(8,128)S(1)} %broadcast_in_dim.22.j_ref), custom_call_target="tpu_custom_call" | custom-call | flops 16056320 | bytes 12845056 | tf_op jit(solution)/shard_map/pallas_call | solution.py:151
  127.2 7.7 %copy.14 = f32[1,1,32,196,256]{4,2,3,1,0:T(8,128)} copy(f32[1,1,32,196,256]{4,3,2,1,0:T(8,128)} %bitcast.11) | data formatting | bytes 12845056 | tf_op jit(solution)/shard_map/reshape | solution.py:192
  (4 shorter events, 0.0 us)
Async XLA Ops:
  2.5 11.2 %copy-start.4 = (f32[2,256]{1,0:T(2,128)S(1)}, f32[2,256]{1,0:T(2,128)}, u32[]{:S(2)}) copy-start(f32[2,256]{1,0:T(2,128)} %param.13) | copy-start | bytes 6148
  2.5 11.2 %copy-start.5 = (f32[2,256]{1,0:T(2,128)S(1)}, f32[2,256]{1,0:T(2,128)}, u32[]{:S(2)}) copy-start(f32[2,256]{1,0:T(2,128)} %param.15) | copy-start | bytes 6148
  13.8 2.4 %copy-start = (bf16[2,9,256,256]{3,2,1,0:T(8,128)(2,1)S(1)}, bf16[2,9,256,256]{3,2,1,0:T(8,128)(2,1)}, u32[]{:S(2)}) copy-start(bf16[2,9,256,256]{3,2,1,0:T(8,128)(2,1)} %param.14) | copy-start | bytes 7077892
  13.8 3.1 %copy-start.1 = (bf16[2,1024,256]{2,1,0:T(8,128)(2,1)S(1)}, bf16[2,1024,256]{2,1,0:T(8,128)(2,1)}, u32[]{:S(2)}) copy-start(bf16[2,1024,256]{2,1,0:T(8,128)(2,1)} %wr_ref.1) | copy-start | bytes 3145732
  13.8 3.4 %copy-start.2 = (bf16[2,256,1024]{2,1,0:T(8,128)(2,1)S(1)}, bf16[2,256,1024]{2,1,0:T(8,128)(2,1)}, u32[]{:S(2)}) copy-start(bf16[2,256,1024]{2,1,0:T(8,128)(2,1)} %we_ref.1) | copy-start | bytes 3145732
  13.8 3.5 %copy-start.3 = (bf16[1024,256]{1,0:T(8,128)(2,1)S(1)}, bf16[1024,256]{1,0:T(8,128)(2,1)}, u32[]{:S(2)}) copy-start(bf16[1024,256]{1,0:T(8,128)(2,1)} %pw_ref.1) | copy-start | bytes 1572868
  106.5 4.4 %collective-permute-start = (f32[4,14,256]{2,1,0:T(8,128)S(1)}, f32[4,14,256]{2,1,0:T(8,128)S(1)}, u32[]{:S(2)}, u32[]{:S(2)}) collective-permute-start(f32[4,14,256]{2,1,0:T(8,128)S(1)} %get-tuple-element.6), channel_id=1, source_target_pairs={{0,1},{1,2},{2,3},{4,5},{5,6},{6,7},{8,9},{9,10},{10,11},{12,13},{... | collective-permute-start | bytes 172040 | tf_op jit(solution)/shard_map/ppermute | solution.py:189
  108.5 7.1 %collective-permute-start.1 = (f32[4,14,256]{2,1,0:T(8,128)S(1)}, f32[4,14,256]{2,1,0:T(8,128)S(1)}, u32[]{:S(2)}, u32[]{:S(2)}) collective-permute-start(f32[4,14,256]{2,1,0:T(8,128)S(1)} %get-tuple-element.5), channel_id=1, source_target_pairs={{1,0},{2,1},{3,2},{5,4},{6,5},{7,6},{9,8},{10,9},{11,10},{13,12},{... | collective-permute-start | bytes 172040 | tf_op jit(solution)/shard_map/ppermute | solution.py:190

commit v2 on v1

v2 whole, which is shorter than its diff:
```python
import jax
import jax.numpy as jnp
from jax import lax
from jax.experimental import pallas as pl
from jax.experimental.pallas import tpu as pltpu
from jax.sharding import PartitionSpec as P

CHAN = 1024
MID = 256
TILE = 14
BLOCKS = 2
TCOLS = 4
CELLS = TILE * TILE
WIDE = 16
PADDED = TILE * WIDE


GROUP = 16
SPAN = 2 * TILE
ROWS = SPAN * GROUP
EDGE = TILE * GROUP


def cell_kernel(
    count_ref, x_ref, m_ref, wr_ref, br_ref, ws_ref, bs_ref, we_ref, pw_ref, o_ref,
    cur_ref, r_ref, c_ref,
):
    g = pl.program_id(0)
    total = CELLS * GROUP
    chunks = CELLS // SPAN

    @pl.when(g * GROUP >= count_ref[0])
    def _():
        o_ref[...] = jnp.zeros(o_ref.shape, o_ref.dtype)

    @pl.when(g * GROUP < count_ref[0])
    def _():
        r_ref[0:GROUP, :] = jnp.zeros((GROUP, MID), jnp.float32)
        r_ref[GROUP + total :, :] = jnp.zeros((GROUP, MID), jnp.float32)
        c_ref[0:EDGE, :] = jnp.zeros((EDGE, 3 * MID), jnp.bfloat16)
        c_ref[EDGE + total :, :] = jnp.zeros((EDGE, 3 * MID), jnp.bfloat16)
        lane = lax.broadcasted_iota(jnp.int32, (SPAN, GROUP, MID), 0)
        keep_left = (lane != 0) & (lane != TILE)
        keep_right = (lane != TILE - 1) & (lane != SPAN - 1)

        def source(b, q0):
            if b == 0:
                return x_ref[pl.ds(q0 // GROUP, SPAN)].reshape(ROWS, CHAN)
            return cur_ref[pl.ds(q0, ROWS), :]

        for b in range(BLOCKS):
            for ch in range(chunks):
                q0 = ch * ROWS
                r = jnp.dot(source(b, q0), wr_ref[b], preferred_element_type=jnp.float32)
                r_ref[pl.ds(GROUP + q0, ROWS), :] = jnp.maximum(r + br_ref[b], 0.0)
            for ch in range(chunks):
                q0 = ch * ROWS
                left = r_ref[pl.ds(q0, ROWS), :].reshape(SPAN, GROUP, MID)
                centre = r_ref[pl.ds(GROUP + q0, ROWS), :]
                right = r_ref[pl.ds(2 * GROUP + q0, ROWS), :].reshape(SPAN, GROUP, MID)
                left = jnp.where(keep_left, left, 0.0).reshape(ROWS, MID)
                right = jnp.where(keep_right, right, 0.0).reshape(ROWS, MID)
                c_ref[pl.ds(EDGE + q0, ROWS), 0:MID] = left.astype(jnp.bfloat16)
                c_ref[pl.ds(EDGE + q0, ROWS), MID : 2 * MID] = centre.astype(jnp.bfloat16)
                c_ref[pl.ds(EDGE + q0, ROWS), 2 * MID :] = right.astype(jnp.bfloat16)
            for ch in range(chunks):
                q0 = ch * ROWS
                acc = jnp.dot(c_ref[pl.ds(q0, ROWS), :], ws_ref[b, 0], preferred_element_type=jnp.float32)
                acc += jnp.dot(c_ref[pl.ds(EDGE + q0, ROWS), :], ws_ref[b, 1], preferred_element_type=jnp.float32)
                acc += jnp.dot(c_ref[pl.ds(2 * EDGE + q0, ROWS), :], ws_ref[b, 2], preferred_element_type=jnp.float32)
                spatial = jnp.maximum(acc + bs_ref[b], 0.0).astype(jnp.bfloat16)
                e = jnp.dot(spatial, we_ref[b], preferred_element_type=jnp.float32)
                res = source(b, q0).astype(jnp.float32)
                cur_ref[pl.ds(q0, ROWS), :] = jnp.maximum(res + e, 0.0).astype(jnp.bfloat16)
        for ch in range(chunks):
            q0 = ch * ROWS
            proj = jnp.dot(cur_ref[pl.ds(q0, ROWS), :], pw_ref[...], preferred_element_type=jnp.float32)
            c0 = ch * SPAN
            o_ref[pl.ds(c0, SPAN)] = proj.reshape(SPAN, GROUP, -1) * m_ref[pl.ds(c0, SPAN)]


def cell_features(count, xt, weight, w_reduce, b_reduce, w_spatial, b_spatial, w_expand, proj_w):
    cells, slots, _ = xt.shape
    emb = proj_w.shape[1]
    ws = w_spatial.reshape(BLOCKS, 3, 3 * MID, MID)
    br = b_reduce.reshape(BLOCKS, 1, MID)
    bs = b_spatial.reshape(BLOCKS, 1, MID)

    def live(g, c):
        return (0, jnp.maximum(jnp.minimum(g, (c[0] - 1) // GROUP), 0), 0)

    def whole(nd):
        return lambda g, c: (0,) * nd

    once = pl.Buffered(1)
    grid_spec = pltpu.PrefetchScalarGridSpec(
        num_scalar_prefetch=1,
        grid=(slots // GROUP,),
        in_specs=[
            pl.BlockSpec((cells, GROUP, CHAN), live),
            pl.BlockSpec((cells, GROUP, 1), lambda g, c: (0, g, 0)),
            pl.BlockSpec((BLOCKS, CHAN, MID), whole(3), pipeline_mode=once),
            pl.BlockSpec((BLOCKS, 1, MID), whole(3), pipeline_mode=once),
            pl.BlockSpec((BLOCKS, 3, 3 * MID, MID), whole(4), pipeline_mode=once),
            pl.BlockSpec((BLOCKS, 1, MID), whole(3), pipeline_mode=once),
            pl.BlockSpec((BLOCKS, MID, CHAN), whole(3), pipeline_mode=once),
            pl.BlockSpec((CHAN, emb), whole(2), pipeline_mode=once),
        ],
        out_specs=pl.BlockSpec((cells, GROUP, emb), lambda g, c: (0, g, 0)),
        scratch_shapes=[
            pltpu.VMEM((cells * GROUP, CHAN), jnp.bfloat16),
            pltpu.VMEM((cells * GROUP + 2 * GROUP, MID), jnp.float32),
            pltpu.VMEM((cells * GROUP + 2 * EDGE, 3 * MID), jnp.bfloat16),
        ],
    )
    flops = 2 * slots * cells * (BLOCKS * (2 * CHAN * MID + 9 * MID * MID) + CHAN * emb)
    return pl.pallas_call(
        cell_kernel,
        grid_spec=grid_spec,
        out_shape=jax.ShapeDtypeStruct((cells, slots, emb), jnp.float32),
        compiler_params=pltpu.CompilerParams(
            dimension_semantics=("arbitrary",), vmem_limit_bytes=60 * 1024 * 1024
        ),
        cost_estimate=pl.CostEstimate(
            flops=flops, transcendentals=0, bytes_accessed=slots * cells * (2 * CHAN + 4 * emb + 4)
        ),
    )(count, xt, weight, w_reduce, br, ws, bs, w_expand, proj_w)


GUARD = 16


def box_kernel(w_ref, hu_ref, hd_ref, j_ref, o_ref, g_ref, v_ref):
    tr = pl.program_id(0)
    rows = pl.num_programs(0)
    col = j_ref[...]
    for tc in range(TCOLS):
        t = tr * TCOLS + tc
        g_ref[TILE : TILE + CELLS, :] = w_ref[t]

        @pl.when(tr == 0)
        def _():
            g_ref[0:TILE, :] = hu_ref[tc]

        @pl.when(tr > 0)
        def _():
            g_ref[0:TILE, :] = w_ref[t - TCOLS, CELLS - TILE : CELLS, :]

        @pl.when(tr == rows - 1)
        def _():
            g_ref[TILE + CELLS : 2 * TILE + CELLS, :] = hd_ref[tc]

        @pl.when(tr < rows - 1)
        def _():
            g_ref[TILE + CELLS : 2 * TILE + CELLS, :] = w_ref[t + TCOLS, 0:TILE, :]

        v = g_ref[0:CELLS, :] + g_ref[TILE : TILE + CELLS, :] + g_ref[2 * TILE : 2 * TILE + CELLS, :]
        v_ref[tc, GUARD : GUARD + CELLS, :] = v
    for tc in range(TCOLS):
        h = v_ref[tc, GUARD : GUARD + CELLS, :]
        h = h + jnp.where(col != 0, v_ref[tc, GUARD - 1 : GUARD - 1 + CELLS, :], 0.0)
        h = h + jnp.where(col != TILE - 1, v_ref[tc, GUARD + 1 : GUARD + 1 + CELLS, :], 0.0)
        if tc > 0:
            h = h + jnp.where(col == 0, v_ref[tc - 1, GUARD + TILE - 1 : GUARD + TILE - 1 + CELLS, :], 0.0)
        if tc < TCOLS - 1:
            h = h + jnp.where(
                col == TILE - 1, v_ref[tc + 1, GUARD - TILE + 1 : GUARD - TILE + 1 + CELLS, :], 0.0
            )
        o_ref[tc] = h / 9.0


def box_average(w, up, down):
    slots, cells, emb = w.shape
    rows = slots // TCOLS
    col = jnp.broadcast_to((jnp.arange(cells, dtype=jnp.int32) % TILE)[:, None], (cells, emb))
    return pl.pallas_call(
        box_kernel,
        grid=(rows,),
        in_specs=[
            pl.BlockSpec((slots, cells, emb), lambda r: (0, 0, 0)),
            pl.BlockSpec((TCOLS, TILE, emb), lambda r: (0, 0, 0)),
            pl.BlockSpec((TCOLS, TILE, emb), lambda r: (0, 0, 0)),
            pl.BlockSpec((cells, emb), lambda r: (0, 0)),
        ],
        out_specs=pl.BlockSpec((TCOLS, cells, emb), lambda r: (r, 0, 0)),
        out_shape=jax.ShapeDtypeStruct(w.shape, jnp.float32),
        scratch_shapes=[
            pltpu.VMEM((2 * TILE + CELLS, emb), jnp.float32),
            pltpu.VMEM((TCOLS, 2 * GUARD + CELLS, emb), jnp.float32),
        ],
        compiler_params=pltpu.CompilerParams(
            dimension_semantics=("arbitrary",), vmem_limit_bytes=48 * 1024 * 1024
        ),
        cost_estimate=pl.CostEstimate(
            flops=10 * slots * cells * emb, transcendentals=0, bytes_accessed=8 * slots * cells * emb
        ),
    )(w, up, down, col)


def per_device(
    tiles, counts, tissue_mask, w_reduce, b_reduce, w_spatial, b_spatial, w_expand, proj_w
):
    slots = tiles.shape[2]
    held = counts[0]
    positions = jnp.arange(slots, dtype=jnp.int32)
    alive = positions < held[0]
    weight = jnp.where(alive[:, None], tissue_mask[0, 0], 0).astype(jnp.float32)
    computed = cell_features(
        held,
        jnp.transpose(tiles[0, 0], (1, 0, 2)),
        weight.T[:, :, None],
        w_reduce,
        b_reduce,
        w_spatial,
        b_spatial,
        w_expand,
        proj_w,
    )
    weighted = jnp.transpose(computed, (1, 0, 2))
    count = lax.axis_size("region")
    forward = [(i, i + 1) for i in range(count - 1)]
    backward = [(target, source) for source, target in forward]
    up = lax.ppermute(weighted[slots - TCOLS :, CELLS - TILE :], "region", forward)
    down = lax.ppermute(weighted[:TCOLS, :TILE], "region", backward)
    averaged = box_average(weighted, up, down)
    return averaged.reshape(1, 1, slots, CELLS, -1)


def solution(mesh):
    placed = (
        P("slide", "region", None, None, None),
        P("slide", "region"),
        P("slide", "region", None, None),
        P(),
        P(),
        P(),
        P(),
        P(),
        P(),
    )
    return jax.shard_map(
        per_device,
        mesh=mesh,
        in_specs=placed,
        out_specs=P("slide", "region", None, None, None),
        check_vma=False,
    )
```

time: 136 us -> 102 us (0.75)
  the two profiles are of different devices: /device:TPU:15 before, /device:TPU:1 now
where the time goes in v2:
time: 102 us; the launch traced here: 101 us
  Pallas kernels  70.3 us (69%)
  local copies, waits for them, and re-layouts  19.9 us (20%)
  starting transfers between devices  8.12 us (8%)
  waiting for transfers between devices  1.29 us (1%)
    pallas_call x1, Pallas kernels, cell_features(): pl.pallas_call(cell_kernel, grid_spec=grid_spec, out_shape=jax.ShapeDtype...  58.8 us
    pallas_call x1, Pallas kernels, box_average(): pl.pallas_call(box_kernel, grid=(rows,), in_specs=[pl.BlockSpec((slots, c...  11.6 us
    reshape x1, local copies, waits for them, and re-layouts, per_device(): return averaged.reshape(1, 1, slots, CELLS, -1)  7.67 us
    pallas_call x1, local copies, waits for them, and re-layouts, cell_features(): pl.pallas_call(cell_kernel, grid_spec=grid_spec, out_shape=jax.ShapeDtype...  6.54 us
    ppermute x1, starting transfers between devices, per_device(): lax.ppermute(weighted[slots - TCOLS:, CELLS - TILE:], 'region', forward)  4.83 us
    ppermute x1, starting transfers between devices, per_device(): down = lax.ppermute(weighted[:TCOLS, :TILE], 'region', backward)  3.29 us
    broadcast_in_dim x1, local copies, waits for them, and re-layouts, per_device(): weight.T[:, :, None]  3.11 us
  transfers between devices with their start and end apart: 2, of which 1 were waited for; matrix products, arithmetic and copies ran while one was open for 0% of the time, Pallas kernels for 0%

profile of v2, /device:TPU:1, one launch (start us, length us, event | category | flops | bytes accessed | tf_op | source)
XLA Modules:
  0.0 101.2 jit_solution(8224044813336835298)
XLA Ops:
  0.7 1.2 %reshape.25.br_ref = f32[2,1,256]{2,1,0:T(1,128)} reshape(f32[2,256]{1,0:T(2,128)} %param.13) | data formatting | bytes 4096 | tf_op jit(solution)/shard_map/reshape | solution.py:86
  1.9 1.2 %reshape.27.bs_ref = f32[2,1,256]{2,1,0:T(1,128)} reshape(f32[2,256]{1,0:T(2,128)} %param.15) | data formatting | bytes 4096 | tf_op jit(solution)/shard_map/reshape | solution.py:87
  3.1 0.8 fusion.1
  3.9 3.1 %copy.13.m_ref = f32[196,32,1]{2,1,0:T(8,128)} copy(f32[196,32,1]{0,1,2:T(8,128)S(1)} %fusion.1) | data formatting | bytes 50176 | tf_op jit(solution)/shard_map/broadcast_in_dim | solution.py:211
  7.1 58.8 %shard_map.91 = f32[196,32,256]{2,1,0:T(8,128)} custom-call(s32[1]{0:T(128)} %bitcast.20.count_ref, bf16[196,32,1024]{2,1,0:T(8,128)(2,1)} %bitcast.25, f32[196,32,1]{2,1,0:T(8,128)} %copy.13.m_ref, bf16[2,1024,256]{2,1,0:T(8,128)(2,1)} %wr_ref.1, f32[2,1,256]{2,1,0:T(1,128)} %reshape.25.br_ref, bf16[2,3,768,256]{3,2,1,0:T(8,128)(2,1)} %bitcast.26, ...), custom_call_target="tpu_custom_call" | custom-call | flops 31239176192 | bytes 19292672 | tf_op jit(solution)/shard_map/pallas_call | solution.py:117
  65.8 6.5 %copy.17 = f32[196,32,256]{2,0,1:T(8,128)S(1)} copy(f32[196,32,256]{2,1,0:T(8,128)} %shard_map.91) | data formatting | bytes 12845056 | tf_op jit(solution)/shard_map/pallas_call | solution.py:117
  72.4 0.0 copy-start
  72.4 3.3 %collective-permute-start.1 = (f32[4,14,256]{2,1,0:T(8,128)S(1)}, f32[4,14,256]{2,1,0:T(8,128)S(1)}, u32[]{:S(2)}, u32[]{:S(2)}) collective-permute-start(f32[4,14,256]{2,1,0:T(8,128)S(1)} %get-tuple-element.5), channel_id=1, source_target_pairs={{1,0},{2,1},{3,2},{5,4},{6,5},{7,6},{9,8},{10,9},{11,10},{13,12},{... | collective-permute-start | bytes 172040 | tf_op jit(solution)/shard_map/ppermute | solution.py:224
  75.7 4.8 %collective-permute-start = (f32[4,14,256]{2,1,0:T(8,128)S(1)}, f32[4,14,256]{2,1,0:T(8,128)S(1)}, u32[]{:S(2)}, u32[]{:S(2)}) collective-permute-start(f32[4,14,256]{2,1,0:T(8,128)S(1)} %get-tuple-element.6), channel_id=1, source_target_pairs={{0,1},{1,2},{2,3},{4,5},{5,6},{6,7},{8,9},{9,10},{10,11},{12,13},{... | collective-permute-start | bytes 172040 | tf_op jit(solution)/shard_map/ppermute | solution.py:223
  80.6 0.0 collective-permute-done.1.hd_ref
  80.6 1.3 %collective-permute-done.hu_ref = f32[4,14,256]{2,1,0:T(8,128)S(1)} collective-permute-done((f32[4,14,256]{2,1,0:T(8,128)S(1)}, f32[4,14,256]{2,1,0:T(8,128)S(1)}, u32[]{:S(2)}, u32[]{:S(2)}) %collective-permute-start) | collective-permute-done | bytes 57376 | tf_op jit(solution)/shard_map/ppermute | solution.py:223
  81.9 0.1 broadcast_in_dim.25.j_ref
  81.9 0.0 copy-done
  82.0 11.6 %shard_map.92 = f32[32,196,256]{2,1,0:T(8,128)} custom-call(f32[32,196,256]{2,1,0:T(8,128)} %bitcast.23, f32[4,14,256]{2,1,0:T(8,128)S(1)} %collective-permute-done.hu_ref, f32[4,14,256]{2,1,0:T(8,128)S(1)} %collective-permute-done.1.hd_ref, s32[196,256]{1,0:T(8,128)S(1)} %broadcast_in_dim.25.j_ref), custom_call_target="tpu_custom_call" | custom-call | flops 16056320 | bytes 12845056 | tf_op jit(solution)/shard_map/pallas_call | solution.py:176
  93.5 7.7 %copy.15 = f32[1,1,32,196,256]{4,2,3,1,0:T(8,128)} copy(f32[1,1,32,196,256]{4,3,2,1,0:T(8,128)} %bitcast.24) | data formatting | bytes 12845056 | tf_op jit(solution)/shard_map/reshape | solution.py:226
  (3 shorter events, 0.0 us)
Async XLA Ops:
  72.4 9.6 %copy-start = (f32[196,32,256]{2,0,1:T(8,128)}, f32[196,32,256]{2,0,1:T(8,128)S(1)}, u32[]{:S(2)}) copy-start(f32[196,32,256]{2,0,1:T(8,128)S(1)} %copy.17) | copy-start | bytes 19267588
  72.4 8.2 %collective-permute-start.1 = (f32[4,14,256]{2,1,0:T(8,128)S(1)}, f32[4,14,256]{2,1,0:T(8,128)S(1)}, u32[]{:S(2)}, u32[]{:S(2)}) collective-permute-start(f32[4,14,256]{2,1,0:T(8,128)S(1)} %get-tuple-element.5), channel_id=1, source_target_pairs={{1,0},{2,1},{3,2},{5,4},{6,5},{7,6},{9,8},{10,9},{11,10},{13,12},{... | collective-permute-start | bytes 172040 | tf_op jit(solution)/shard_map/ppermute | solution.py:224
  75.7 6.1 %collective-permute-start = (f32[4,14,256]{2,1,0:T(8,128)S(1)}, f32[4,14,256]{2,1,0:T(8,128)S(1)}, u32[]{:S(2)}, u32[]{:S(2)}) collective-permute-start(f32[4,14,256]{2,1,0:T(8,128)S(1)} %get-tuple-element.6), channel_id=1, source_target_pairs={{0,1},{1,2},{2,3},{4,5},{5,6},{6,7},{8,9},{9,10},{10,11},{12,13},{... | collective-permute-start | bytes 172040 | tf_op jit(solution)/shard_map/ppermute | solution.py:223

commit v3 on v2

--- a/solution.py
+++ b/solution.py
@@ -127,74 +127,55 @@
     )(count, xt, weight, w_reduce, br, ws, bs, w_expand, proj_w)
 
 
-GUARD = 16
-
-
-def box_kernel(w_ref, hu_ref, hd_ref, j_ref, o_ref, g_ref, v_ref):
-    tr = pl.program_id(0)
-    rows = pl.num_programs(0)
-    col = j_ref[...]
-    for tc in range(TCOLS):
-        t = tr * TCOLS + tc
-        g_ref[TILE : TILE + CELLS, :] = w_ref[t]
-
-        @pl.when(tr == 0)
-        def _():
-            g_ref[0:TILE, :] = hu_ref[tc]
-
-        @pl.when(tr > 0)
-        def _():
-            g_ref[0:TILE, :] = w_ref[t - TCOLS, CELLS - TILE : CELLS, :]
-
-        @pl.when(tr == rows - 1)
-        def _():
-            g_ref[TILE + CELLS : 2 * TILE + CELLS, :] = hd_ref[tc]
-
-        @pl.when(tr < rows - 1)
-        def _():
-            g_ref[TILE + CELLS : 2 * TILE + CELLS, :] = w_ref[t + TCOLS, 0:TILE, :]
-
-        v = g_ref[0:CELLS, :] + g_ref[TILE : TILE + CELLS, :] + g_ref[2 * TILE : 2 * TILE + CELLS, :]
-        v_ref[tc, GUARD : GUARD + CELLS, :] = v
-    for tc in range(TCOLS):
-        h = v_ref[tc, GUARD : GUARD + CELLS, :]
-        h = h + jnp.where(col != 0, v_ref[tc, GUARD - 1 : GUARD - 1 + CELLS, :], 0.0)
-        h = h + jnp.where(col != TILE - 1, v_ref[tc, GUARD + 1 : GUARD + 1 + CELLS, :], 0.0)
-        if tc > 0:
-            h = h + jnp.where(col == 0, v_ref[tc - 1, GUARD + TILE - 1 : GUARD + TILE - 1 + CELLS, :], 0.0)
-        if tc < TCOLS - 1:
-            h = h + jnp.where(
-                col == TILE - 1, v_ref[tc + 1, GUARD - TILE + 1 : GUARD - TILE + 1 + CELLS, :], 0.0
-            )
-        o_ref[tc] = h / 9.0
-
-
-def box_average(w, up, down):
-    slots, cells, emb = w.shape
-    rows = slots // TCOLS
-    col = jnp.broadcast_to((jnp.arange(cells, dtype=jnp.int32) % TILE)[:, None], (cells, emb))
-    return pl.pallas_call(
-        box_kernel,
-        grid=(rows,),
-        in_specs=[
-            pl.BlockSpec((slots, cells, emb), lambda r: (0, 0, 0)),
-            pl.BlockSpec((TCOLS, TILE, emb), lambda r: (0, 0, 0)),
-            pl.BlockSpec((TCOLS, TILE, emb), lambda r: (0, 0, 0)),
-            pl.BlockSpec((cells, emb), lambda r: (0, 0)),
+def grid_box_kernel(w_ref, hu_ref, hd_ref, o_ref, v_ref, ub_ref, db_ref, sh_ref):
+    slots = w_ref.shape[2]
+    ub_ref[:, 8 : 8 + slots, :] = w_ref[TILE - 1]
+    ub_ref[:, 4:8, :] = hu_ref[...]
+    db_ref[:, 0:slots, :] = w_ref[0]
+    db_ref[:, slots : slots + 4, :] = hd_ref[...]
+    v_ref[0] = ub_ref[:, 4 : 4 + slots, :] + w_ref[0] + w_ref[1]
+    v_ref[TILE - 1] = w_ref[TILE - 2] + w_ref[TILE - 1] + db_ref[:, 4 : 4 + slots, :]
+
+    def vertical(i, carry):
+        v_ref[i] = w_ref[i - 1] + w_ref[i] + w_ref[i + 1]
+        return carry
+
+    lax.fori_loop(1, TILE - 1, vertical, 0)
+    slot = lax.broadcasted_iota(jnp.int32, (slots, w_ref.shape[3]), 0) & (TCOLS - 1)
+
+    def horizontal(i, carry):
+        o_ref[i, 1 : TILE - 1] = (
+            v_ref[i, 0 : TILE - 2] + v_ref[i, 1 : TILE - 1] + v_ref[i, 2:TILE]
+        ) / 9.0
+        sh_ref[8 : 8 + slots, :] = v_ref[i, TILE - 1]
+        left = jnp.where(slot != 0, sh_ref[7 : 7 + slots, :], 0.0)
+        o_ref[i, 0] = (left + v_ref[i, 0] + v_ref[i, 1]) / 9.0
+        sh_ref[8 : 8 + slots, :] = v_ref[i, 0]
+        right = jnp.where(slot != TCOLS - 1, sh_ref[9 : 9 + slots, :], 0.0)
+        o_ref[i, TILE - 1] = (v_ref[i, TILE - 2] + v_ref[i, TILE - 1] + right) / 9.0
+        return carry
+
+    lax.fori_loop(0, TILE, horizontal, 0)
+
+
+def grid_box_average(w, up, down):
+    cells, slots, emb = w.shape
+    w4 = w.reshape(TILE, TILE, slots, emb)
+    out = pl.pallas_call(
+        grid_box_kernel,
+        out_shape=jax.ShapeDtypeStruct(w4.shape, jnp.float32),
+        scratch_shapes=[
+            pltpu.VMEM(w4.shape, jnp.float32),
+            pltpu.VMEM((TILE, slots + 8, emb), jnp.float32),
+            pltpu.VMEM((TILE, slots + 8, emb), jnp.float32),
+            pltpu.VMEM((slots + 16, emb), jnp.float32),
         ],
-        out_specs=pl.BlockSpec((TCOLS, cells, emb), lambda r: (r, 0, 0)),
-        out_shape=jax.ShapeDtypeStruct(w.shape, jnp.float32),
-        scratch_shapes=[
-            pltpu.VMEM((2 * TILE + CELLS, emb), jnp.float32),
-            pltpu.VMEM((TCOLS, 2 * GUARD + CELLS, emb), jnp.float32),
-        ],
-        compiler_params=pltpu.CompilerParams(
-            dimension_semantics=("arbitrary",), vmem_limit_bytes=48 * 1024 * 1024
-        ),
+        compiler_params=pltpu.CompilerParams(vmem_limit_bytes=48 * 1024 * 1024),
         cost_estimate=pl.CostEstimate(
             flops=10 * slots * cells * emb, transcendentals=0, bytes_accessed=8 * slots * cells * emb
         ),
-    )(w, up, down, col)
+    )(w4, up, down)
+    return out.reshape(cells, slots, emb)
 
 
 def per_device(
@@ -216,14 +197,13 @@
         w_expand,
         proj_w,
     )
-    weighted = jnp.transpose(computed, (1, 0, 2))
     count = lax.axis_size("region")
     forward = [(i, i + 1) for i in range(count - 1)]
     backward = [(target, source) for source, target in forward]
-    up = lax.ppermute(weighted[slots - TCOLS :, CELLS - TILE :], "region", forward)
-    down = lax.ppermute(weighted[:TCOLS, :TILE], "region", backward)
-    averaged = box_average(weighted, up, down)
-    return averaged.reshape(1, 1, slots, CELLS, -1)
+    up = lax.ppermute(computed[CELLS - TILE :, slots - TCOLS :], "region", forward)
+    down = lax.ppermute(computed[:TILE, :TCOLS], "region", backward)
+    averaged = grid_box_average(computed, up, down)
+    return jnp.transpose(averaged, (1, 0, 2)).reshape(1, 1, slots, CELLS, -1)
 
 
 def solution(mesh):

time: 102 us -> 84.9 us (0.83)
  local copies, waits for them, and re-layouts: 19.9 us -> 6.5 us
  Pallas kernels: 70.3 us -> 67 us
  starting transfers between devices: 8.12 us -> 7.07 us
    reshape x1 -> x0, local copies, waits for them, and re-layouts: 7.67 us -> none  [per_device(): return averaged.reshape(1, 1, slots, CELLS, -1)]
    pallas_call x1 -> x0, local copies, waits for them, and re-layouts: 6.54 us -> none  [cell_features(): pl.pallas_call(cell_kernel, grid_spec=grid_spec, out_shape=jax.ShapeDtype...]
    pallas_call x1, Pallas kernels: 11.6 us -> 8.13 us  [grid_box_average(): pl.pallas_call(grid_box_kernel, out_shape=jax.ShapeDtypeStruct(w4.shape,...]
    ppermute x2, starting transfers between devices: 8.12 us -> 7.07 us  [the longest x1 5.15 us: per_device(): lax.ppermute(computed[CELLS - TILE:, slots - TCOLS:], 'region', forward)]
where the time goes in v3:
time: 84.9 us; the launch traced here: 83.3 us
  Pallas kernels  67 us (79%)
  starting transfers between devices  7.07 us (8%)
  local copies, waits for them, and re-layouts  6.5 us (8%)
  waiting for transfers between devices  1.23 us (1%)
    pallas_call x1, Pallas kernels, cell_features(): pl.pallas_call(cell_kernel, grid_spec=grid_spec, out_shape=jax.ShapeDtype...  58.9 us
    pallas_call x1, Pallas kernels, grid_box_average(): pl.pallas_call(grid_box_kernel, out_shape=jax.ShapeDtypeStruct(w4.shape,...  8.13 us
    ppermute x1, starting transfers between devices, per_device(): lax.ppermute(computed[CELLS - TILE:, slots - TCOLS:], 'region', forward)  5.15 us
    broadcast_in_dim x1, local copies, waits for them, and re-layouts, per_device(): weight.T[:, :, None]  3 us
    ppermute x1, starting transfers between devices, per_device(): down = lax.ppermute(computed[:TILE, :TCOLS], 'region', backward)  1.92 us
  transfers between devices with their start and end apart: 2, of which 1 were waited for; matrix products, arithmetic and copies ran while one was open for 0% of the time, Pallas kernels for 0%

profile of v3, /device:TPU:1, one launch (start us, length us, event | category | flops | bytes accessed | tf_op | source)
XLA Modules:
  0.0 83.3 jit_solution(5123165985835465311)
XLA Ops:
  0.7 1.3 %reshape.22.br_ref = f32[2,1,256]{2,1,0:T(1,128)} reshape(f32[2,256]{1,0:T(2,128)} %param.13) | data formatting | bytes 4096 | tf_op jit(solution)/shard_map/reshape | solution.py:86
  1.9 1.3 %reshape.24.bs_ref = f32[2,1,256]{2,1,0:T(1,128)} reshape(f32[2,256]{1,0:T(2,128)} %param.15) | data formatting | bytes 4096 | tf_op jit(solution)/shard_map/reshape | solution.py:87
  3.2 0.8 fusion.1
  4.0 3.0 %copy.11.m_ref = f32[196,32,1]{2,1,0:T(8,128)} copy(f32[196,32,1]{0,1,2:T(8,128)S(1)} %fusion.1) | data formatting | bytes 50176 | tf_op jit(solution)/shard_map/broadcast_in_dim | solution.py:192
  7.0 58.9 %shard_map.91 = f32[196,32,256]{2,1,0:T(8,128)} custom-call(s32[1]{0:T(128)} %bitcast.22.count_ref, bf16[196,32,1024]{2,1,0:T(8,128)(2,1)} %bitcast.25, f32[196,32,1]{2,1,0:T(8,128)} %copy.11.m_ref, bf16[2,1024,256]{2,1,0:T(8,128)(2,1)} %wr_ref.1, f32[2,1,256]{2,1,0:T(1,128)} %reshape.22.br_ref, bf16[2,3,768,256]{3,2,1,0:T(8,128)(2,1)} %bitcast.26, ...), custom_call_target="tpu_custom_call" | custom-call | flops 31239176192 | bytes 19292672 | tf_op jit(solution)/shard_map/pallas_call | solution.py:117
  65.9 1.0 %fusion.2 = (f32[14,4,256]{2,1,0:T(4,128)S(1)}, f32[14,4,256]{2,1,0:T(4,128)S(1)}) fusion(f32[196,32,256]{2,1,0:T(8,128)} %shard_map.91), kind=kLoop, calls=%fused_computation.4 | loop fusion | bytes 229376 | tf_op jit(solution)/shard_map/slice | solution.py:204
  66.9 1.9 %collective-permute-start.1 = (f32[14,4,256]{2,1,0:T(4,128)S(1)}, f32[14,4,256]{2,1,0:T(4,128)S(1)}, u32[]{:S(2)}, u32[]{:S(2)}) collective-permute-start(f32[14,4,256]{2,1,0:T(4,128)S(1)} %get-tuple-element.5), channel_id=1, source_target_pairs={{1,0},{2,1},{3,2},{5,4},{6,5},{7,6},{9,8},{10,9},{11,10},{13,12},{... | collective-permute-start | bytes 172040 | tf_op jit(solution)/shard_map/ppermute | solution.py:204
  68.8 5.1 %collective-permute-start = (f32[14,4,256]{2,1,0:T(4,128)S(1)}, f32[14,4,256]{2,1,0:T(4,128)S(1)}, u32[]{:S(2)}, u32[]{:S(2)}) collective-permute-start(f32[14,4,256]{2,1,0:T(4,128)S(1)} %get-tuple-element.6), channel_id=1, source_target_pairs={{0,1},{1,2},{2,3},{4,5},{5,6},{6,7},{8,9},{9,10},{10,11},{12,13},{... | collective-permute-start | bytes 172040 | tf_op jit(solution)/shard_map/ppermute | solution.py:203
  73.9 0.0 collective-permute-done.1.hd_ref
  73.9 1.2 %collective-permute-done.hu_ref = f32[14,4,256]{2,1,0:T(4,128)S(1)} collective-permute-done((f32[14,4,256]{2,1,0:T(4,128)S(1)}, f32[14,4,256]{2,1,0:T(4,128)S(1)}, u32[]{:S(2)}, u32[]{:S(2)}) %collective-permute-start) | collective-permute-done | bytes 57376 | tf_op jit(solution)/shard_map/ppermute | solution.py:203
  75.2 8.1 %shard_map.92 = f32[14,14,32,256]{3,2,1,0:T(8,128)} custom-call(f32[14,14,32,256]{3,2,1,0:T(8,128)} %bitcast.24, f32[14,4,256]{2,1,0:T(4,128)S(1)} %collective-permute-done.hu_ref, f32[14,4,256]{2,1,0:T(4,128)S(1)} %collective-permute-done.1.hd_ref), custom_call_target="tpu_custom_call" | custom-call | flops 16056320 | bytes 12845056 | tf_op jit(solution)/shard_map/pallas_call | solution.py:164
  (1 shorter events, 0.0 us)
Async XLA Ops:
  66.9 7.1 %collective-permute-start.1 = (f32[14,4,256]{2,1,0:T(4,128)S(1)}, f32[14,4,256]{2,1,0:T(4,128)S(1)}, u32[]{:S(2)}, u32[]{:S(2)}) collective-permute-start(f32[14,4,256]{2,1,0:T(4,128)S(1)} %get-tuple-element.5), channel_id=1, source_target_pairs={{1,0},{2,1},{3,2},{5,4},{6,5},{7,6},{9,8},{10,9},{11,10},{13,12},{... | collective-permute-start | bytes 172040 | tf_op jit(solution)/shard_map/ppermute | solution.py:204
  68.8 6.4 %collective-permute-start = (f32[14,4,256]{2,1,0:T(4,128)S(1)}, f32[14,4,256]{2,1,0:T(4,128)S(1)}, u32[]{:S(2)}, u32[]{:S(2)}) collective-permute-start(f32[14,4,256]{2,1,0:T(4,128)S(1)} %get-tuple-element.6), channel_id=1, source_target_pairs={{0,1},{1,2},{2,3},{4,5},{5,6},{6,7},{8,9},{9,10},{10,11},{12,13},{... | collective-permute-start | bytes 172040 | tf_op jit(solution)/shard_map/ppermute | solution.py:203

commit v4 on v3

--- a/solution.py
+++ b/solution.py
@@ -16,7 +16,7 @@
 
 
 GROUP = 16
-SPAN = 2 * TILE
+SPAN = 7 * TILE
 ROWS = SPAN * GROUP
 EDGE = TILE * GROUP
 
@@ -40,8 +40,11 @@
         c_ref[0:EDGE, :] = jnp.zeros((EDGE, 3 * MID), jnp.bfloat16)
         c_ref[EDGE + total :, :] = jnp.zeros((EDGE, 3 * MID), jnp.bfloat16)
         lane = lax.broadcasted_iota(jnp.int32, (SPAN, GROUP, MID), 0)
-        keep_left = (lane != 0) & (lane != TILE)
-        keep_right = (lane != TILE - 1) & (lane != SPAN - 1)
+        keep_left = lane != 0
+        keep_right = lane != TILE - 1
+        for row in range(1, SPAN // TILE):
+            keep_left = keep_left & (lane != TILE * row)
+            keep_right = keep_right & (lane != TILE * row + TILE - 1)
 
         def source(b, q0):
             if b == 0:

time: 84.9 us -> 84 us (0.989)
  Pallas kernels: 67 us -> 66.1 us
    ppermute x1, starting transfers between devices: 1.92 us -> 3.29 us  [per_device(): down = lax.ppermute(computed[:TILE, :TCOLS], 'region', backward)]
    ppermute x1, starting transfers between devices: 5.15 us -> 3.78 us  [per_device(): lax.ppermute(computed[CELLS - TILE:, slots - TCOLS:], 'region', forward)]
    pallas_call x1, Pallas kernels: 58.9 us -> 57.9 us  [cell_features(): pl.pallas_call(cell_kernel, grid_spec=grid_spec, out_shape=jax.ShapeDtype...]
where the time goes in v4:
time: 84 us; the launch traced here: 82.4 us
  Pallas kernels  66.1 us (79%)
  starting transfers between devices  7.07 us (8%)
  local copies, waits for them, and re-layouts  6.5 us (8%)
  waiting for transfers between devices  1.23 us (1%)
  other arithmetic  0.84 us (1%)
    pallas_call x1, Pallas kernels, cell_features(): pl.pallas_call(cell_kernel, grid_spec=grid_spec, out_shape=jax.ShapeDtype...  57.9 us
    pallas_call x1, Pallas kernels, grid_box_average(): pl.pallas_call(grid_box_kernel, out_shape=jax.ShapeDtypeStruct(w4.shape,...  8.13 us
    ppermute x1, starting transfers between devices, per_device(): lax.ppermute(computed[CELLS - TILE:, slots - TCOLS:], 'region', forward)  3.78 us
    ppermute x1, starting transfers between devices, per_device(): down = lax.ppermute(computed[:TILE, :TCOLS], 'region', backward)  3.29 us
    broadcast_in_dim x1, local copies, waits for them, and re-layouts, per_device(): weight.T[:, :, None]  3 us
  transfers between devices with their start and end apart: 2, of which 1 were waited for; matrix products, arithmetic and copies ran while one was open for 0% of the time, Pallas kernels for 0%

profile of v4, /device:TPU:1, one launch (start us, length us, event | category | flops | bytes accessed | tf_op | source)
XLA Modules:
  0.0 82.4 jit_solution(8499560680960295962)
XLA Ops:
  0.7 1.3 %reshape.22.br_ref = f32[2,1,256]{2,1,0:T(1,128)} reshape(f32[2,256]{1,0:T(2,128)} %param.13) | data formatting | bytes 4096 | tf_op jit(solution)/shard_map/reshape | solution.py:89
  1.9 1.3 %reshape.24.bs_ref = f32[2,1,256]{2,1,0:T(1,128)} reshape(f32[2,256]{1,0:T(2,128)} %param.15) | data formatting | bytes 4096 | tf_op jit(solution)/shard_map/reshape | solution.py:90
  3.2 0.8 %fusion.1 = f32[196,32,1]{0,1,2:T(8,128)S(1)} fusion(s32[1,1,32,196]{3,2,1,0:T(8,128)} %param.11, pred[32]{0:T(512)(128)(4,1)S(1)} %iota_compare_fusion), kind=kLoop, calls=%fused_computation.2 | loop fusion | flops 12544 | bytes 50208 | tf_op jit(solution)/shard_map/broadcast_in_dim | solution.py:195
  4.0 3.0 %copy.11.m_ref = f32[196,32,1]{2,1,0:T(8,128)} copy(f32[196,32,1]{0,1,2:T(8,128)S(1)} %fusion.1) | data formatting | bytes 50176 | tf_op jit(solution)/shard_map/broadcast_in_dim | solution.py:195
  7.0 57.9 %shard_map.91 = f32[196,32,256]{2,1,0:T(8,128)} custom-call(s32[1]{0:T(128)} %bitcast.22.count_ref, bf16[196,32,1024]{2,1,0:T(8,128)(2,1)} %bitcast.25, f32[196,32,1]{2,1,0:T(8,128)} %copy.11.m_ref, bf16[2,1024,256]{2,1,0:T(8,128)(2,1)} %wr_ref.1, f32[2,1,256]{2,1,0:T(1,128)} %reshape.22.br_ref, bf16[2,3,768,256]{3,2,1,0:T(8,128)(2,1)} %bitcast.26, ...), custom_call_target="tpu_custom_call" | custom-call | flops 31239176192 | bytes 19292672 | tf_op jit(solution)/shard_map/pallas_call | solution.py:120
  64.9 1.0 %fusion.2 = (f32[14,4,256]{2,1,0:T(4,128)S(1)}, f32[14,4,256]{2,1,0:T(4,128)S(1)}) fusion(f32[196,32,256]{2,1,0:T(8,128)} %shard_map.91), kind=kLoop, calls=%fused_computation.4 | loop fusion | bytes 229376 | tf_op jit(solution)/shard_map/slice | solution.py:207
  65.9 3.3 %collective-permute-start.1 = (f32[14,4,256]{2,1,0:T(4,128)S(1)}, f32[14,4,256]{2,1,0:T(4,128)S(1)}, u32[]{:S(2)}, u32[]{:S(2)}) collective-permute-start(f32[14,4,256]{2,1,0:T(4,128)S(1)} %get-tuple-element.5), channel_id=1, source_target_pairs={{1,0},{2,1},{3,2},{5,4},{6,5},{7,6},{9,8},{10,9},{11,10},{13,12},{... | collective-permute-start | bytes 172040 | tf_op jit(solution)/shard_map/ppermute | solution.py:207
  69.2 3.8 %collective-permute-start = (f32[14,4,256]{2,1,0:T(4,128)S(1)}, f32[14,4,256]{2,1,0:T(4,128)S(1)}, u32[]{:S(2)}, u32[]{:S(2)}) collective-permute-start(f32[14,4,256]{2,1,0:T(4,128)S(1)} %get-tuple-element.6), channel_id=1, source_target_pairs={{0,1},{1,2},{2,3},{4,5},{5,6},{6,7},{8,9},{9,10},{10,11},{12,13},{... | collective-permute-start | bytes 172040 | tf_op jit(solution)/shard_map/ppermute | solution.py:206
  73.0 0.0 collective-permute-done.1.hd_ref
  73.0 1.2 %collective-permute-done.hu_ref = f32[14,4,256]{2,1,0:T(4,128)S(1)} collective-permute-done((f32[14,4,256]{2,1,0:T(4,128)S(1)}, f32[14,4,256]{2,1,0:T(4,128)S(1)}, u32[]{:S(2)}, u32[]{:S(2)}) %collective-permute-start) | collective-permute-done | bytes 57376 | tf_op jit(solution)/shard_map/ppermute | solution.py:206
  74.2 8.1 %shard_map.92 = f32[14,14,32,256]{3,2,1,0:T(8,128)} custom-call(f32[14,14,32,256]{3,2,1,0:T(8,128)} %bitcast.24, f32[14,4,256]{2,1,0:T(4,128)S(1)} %collective-permute-done.hu_ref, f32[14,4,256]{2,1,0:T(4,128)S(1)} %collective-permute-done.1.hd_ref), custom_call_target="tpu_custom_call" | custom-call | flops 16056320 | bytes 12845056 | tf_op jit(solution)/shard_map/pallas_call | solution.py:167
  (1 shorter events, 0.0 us)
Async XLA Ops:
  65.9 7.1 %collective-permute-start.1 = (f32[14,4,256]{2,1,0:T(4,128)S(1)}, f32[14,4,256]{2,1,0:T(4,128)S(1)}, u32[]{:S(2)}, u32[]{:S(2)}) collective-permute-start(f32[14,4,256]{2,1,0:T(4,128)S(1)} %get-tuple-element.5), channel_id=1, source_target_pairs={{1,0},{2,1},{3,2},{5,4},{6,5},{7,6},{9,8},{10,9},{11,10},{13,12},{... | collective-permute-start | bytes 172040 | tf_op jit(solution)/shard_map/ppermute | solution.py:207
  69.2 5.0 %collective-permute-start = (f32[14,4,256]{2,1,0:T(4,128)S(1)}, f32[14,4,256]{2,1,0:T(4,128)S(1)}, u32[]{:S(2)}, u32[]{:S(2)}) collective-permute-start(f32[14,4,256]{2,1,0:T(4,128)S(1)} %get-tuple-element.6), channel_id=1, source_target_pairs={{0,1},{1,2},{2,3},{4,5},{5,6},{6,7},{8,9},{9,10},{10,11},{12,13},{... | collective-permute-start | bytes 172040 | tf_op jit(solution)/shard_map/ppermute | solution.py:206

commit v5 on v4

--- a/solution.py
+++ b/solution.py
@@ -55,7 +55,7 @@
             for ch in range(chunks):
                 q0 = ch * ROWS
                 r = jnp.dot(source(b, q0), wr_ref[b], preferred_element_type=jnp.float32)
-                r_ref[pl.ds(GROUP + q0, ROWS), :] = jnp.maximum(r + br_ref[b], 0.0)
+                r_ref[pl.ds(GROUP + q0, ROWS), :] = jnp.maximum(r + br_ref[b : b + 1, :], 0.0)
             for ch in range(chunks):
                 q0 = ch * ROWS
                 left = r_ref[pl.ds(q0, ROWS), :].reshape(SPAN, GROUP, MID)
@@ -71,7 +71,7 @@
                 acc = jnp.dot(c_ref[pl.ds(q0, ROWS), :], ws_ref[b, 0], preferred_element_type=jnp.float32)
                 acc += jnp.dot(c_ref[pl.ds(EDGE + q0, ROWS), :], ws_ref[b, 1], preferred_element_type=jnp.float32)
                 acc += jnp.dot(c_ref[pl.ds(2 * EDGE + q0, ROWS), :], ws_ref[b, 2], preferred_element_type=jnp.float32)
-                spatial = jnp.maximum(acc + bs_ref[b], 0.0).astype(jnp.bfloat16)
+                spatial = jnp.maximum(acc + bs_ref[b : b + 1, :], 0.0).astype(jnp.bfloat16)
                 e = jnp.dot(spatial, we_ref[b], preferred_element_type=jnp.float32)
                 res = source(b, q0).astype(jnp.float32)
                 cur_ref[pl.ds(q0, ROWS), :] = jnp.maximum(res + e, 0.0).astype(jnp.bfloat16)
@@ -86,9 +86,6 @@
     cells, slots, _ = xt.shape
     emb = proj_w.shape[1]
     ws = w_spatial.reshape(BLOCKS, 3, 3 * MID, MID)
-    br = b_reduce.reshape(BLOCKS, 1, MID)
-    bs = b_spatial.reshape(BLOCKS, 1, MID)
-
     def live(g, c):
         return (0, jnp.maximum(jnp.minimum(g, (c[0] - 1) // GROUP), 0), 0)
 
@@ -103,9 +100,9 @@
             pl.BlockSpec((cells, GROUP, CHAN), live),
             pl.BlockSpec((cells, GROUP, 1), lambda g, c: (0, g, 0)),
             pl.BlockSpec((BLOCKS, CHAN, MID), whole(3), pipeline_mode=once),
-            pl.BlockSpec((BLOCKS, 1, MID), whole(3), pipeline_mode=once),
+            pl.BlockSpec((BLOCKS, MID), whole(2), pipeline_mode=once),
             pl.BlockSpec((BLOCKS, 3, 3 * MID, MID), whole(4), pipeline_mode=once),
-            pl.BlockSpec((BLOCKS, 1, MID), whole(3), pipeline_mode=once),
+            pl.BlockSpec((BLOCKS, MID), whole(2), pipeline_mode=once),
             pl.BlockSpec((BLOCKS, MID, CHAN), whole(3), pipeline_mode=once),
             pl.BlockSpec((CHAN, emb), whole(2), pipeline_mode=once),
         ],
@@ -127,7 +124,7 @@
         cost_estimate=pl.CostEstimate(
             flops=flops, transcendentals=0, bytes_accessed=slots * cells * (2 * CHAN + 4 * emb + 4)
         ),
-    )(count, xt, weight, w_reduce, br, ws, bs, w_expand, proj_w)
+    )(count, xt, weight, w_reduce, b_reduce, ws, b_spatial, w_expand, proj_w)
 
 
 def grid_box_kernel(w_ref, hu_ref, hd_ref, o_ref, v_ref, ub_ref, db_ref, sh_ref):
@@ -192,7 +189,7 @@
     computed = cell_features(
         held,
         jnp.transpose(tiles[0, 0], (1, 0, 2)),
-        weight.T[:, :, None],
+        weight.T[:, :, None].astype(jnp.bfloat16),
         w_reduce,
         b_reduce,
         w_spatial,

time: 84 us -> 80.7 us (0.961)
  local copies, waits for them, and re-layouts: 6.5 us -> 3.49 us
    broadcast_in_dim x1 -> x0, local copies, waits for them, and re-layouts: 3 us -> none  [per_device(): weight.T[:, :, None]]
    reshape x2 -> x0, local copies, waits for them, and re-layouts: 2.53 us -> none  [the longest x1 1.26 us: cell_features(): br = b_reduce.reshape(BLOCKS, 1, MID)]
    convert_element_type x0 -> x1, local copies, waits for them, and re-layouts: none -> 2.52 us  [per_device(): weight.T[:, :, None].astype(jnp.bfloat16)]
    ppermute x1, starting transfers between devices: 3.78 us -> 5.15 us  [per_device(): lax.ppermute(computed[CELLS - TILE:, slots - TCOLS:], 'region', forward)]
    ppermute x1, starting transfers between devices: 3.29 us -> 1.92 us  [per_device(): down = lax.ppermute(computed[:TILE, :TCOLS], 'region', backward)]
where the time goes in v5:
time: 80.7 us; the launch traced here: 79.1 us
  Pallas kernels  65.8 us (82%)
  starting transfers between devices  7.07 us (9%)
  local copies, waits for them, and re-layouts  3.49 us (4%)
  waiting for transfers between devices  1.23 us (2%)
  other arithmetic  0.84 us (1%)
    pallas_call x1, Pallas kernels, cell_features(): pl.pallas_call(cell_kernel, grid_spec=grid_spec, out_shape=jax.ShapeDtype...  57.7 us
    pallas_call x1, Pallas kernels, grid_box_average(): pl.pallas_call(grid_box_kernel, out_shape=jax.ShapeDtypeStruct(w4.shape,...  8.13 us
    ppermute x1, starting transfers between devices, per_device(): lax.ppermute(computed[CELLS - TILE:, slots - TCOLS:], 'region', forward)  5.15 us
    convert_element_type x1, local copies, waits for them, and re-layouts, per_device(): weight.T[:, :, None].astype(jnp.bfloat16)  2.52 us
    ppermute x1, starting transfers between devices, per_device(): down = lax.ppermute(computed[:TILE, :TCOLS], 'region', backward)  1.92 us
  transfers between devices with their start and end apart: 2, of which 1 were waited for; matrix products, arithmetic and copies ran while one was open for 0% of the time, Pallas kernels for 0%

profile of v5, /device:TPU:1, one launch (start us, length us, event | category | flops | bytes accessed | tf_op | source)
XLA Modules:
  0.0 79.1 jit_solution(4780453148452186653)
XLA Ops:
  0.7 0.8 %fusion.2 = bf16[196,32,1]{0,1,2:T(8,128)(2,1)S(1)} fusion(s32[1,1,32,196]{3,2,1,0:T(8,128)} %param.11, pred[32]{0:T(512)(128)(4,1)S(1)} %iota_compare_fusion), kind=kLoop, calls=%fused_computation.3 | loop fusion | flops 18816 | bytes 37664 | tf_op jit(solution)/shard_map/convert_element_type | solution.py:192
  1.5 2.5 %copy.11.m_ref = bf16[196,32,1]{2,1,0:T(8,128)(2,1)} copy(bf16[196,32,1]{0,1,2:T(8,128)(2,1)S(1)} %fusion.2) | data formatting | bytes 25088 | tf_op jit(solution)/shard_map/convert_element_type | solution.py:192
  4.0 57.7 %shard_map.91 = f32[196,32,256]{2,1,0:T(8,128)} custom-call(s32[1]{0:T(128)} %bitcast.24.count_ref, bf16[196,32,1024]{2,1,0:T(8,128)(2,1)} %bitcast.27, bf16[196,32,1]{2,1,0:T(8,128)(2,1)} %copy.11.m_ref, bf16[2,1024,256]{2,1,0:T(8,128)(2,1)} %wr_ref.1, f32[2,256]{1,0:T(2,128)} %br_ref.1, bf16[2,3,768,256]{3,2,1,0:T(8,128)(2,1)} %bitcast.28, ...), custom_call_target="tpu_custom_call" | custom-call | flops 31239176192 | bytes 19292672 | tf_op jit(solution)/shard_map/pallas_call | solution.py:117
  61.7 1.0 %fusion.3 = (f32[14,4,256]{2,1,0:T(4,128)S(1)}, f32[14,4,256]{2,1,0:T(4,128)S(1)}) fusion(f32[196,32,256]{2,1,0:T(8,128)} %shard_map.91), kind=kLoop, calls=%fused_computation.5 | loop fusion | bytes 229376 | tf_op jit(solution)/shard_map/slice | solution.py:204
  62.6 1.9 %collective-permute-start.1 = (f32[14,4,256]{2,1,0:T(4,128)S(1)}, f32[14,4,256]{2,1,0:T(4,128)S(1)}, u32[]{:S(2)}, u32[]{:S(2)}) collective-permute-start(f32[14,4,256]{2,1,0:T(4,128)S(1)} %get-tuple-element.5), channel_id=1, source_target_pairs={{1,0},{2,1},{3,2},{5,4},{6,5},{7,6},{9,8},{10,9},{11,10},{13,12},{... | collective-permute-start | bytes 172040 | tf_op jit(solution)/shard_map/ppermute | solution.py:204
  64.6 5.1 %collective-permute-start = (f32[14,4,256]{2,1,0:T(4,128)S(1)}, f32[14,4,256]{2,1,0:T(4,128)S(1)}, u32[]{:S(2)}, u32[]{:S(2)}) collective-permute-start(f32[14,4,256]{2,1,0:T(4,128)S(1)} %get-tuple-element.6), channel_id=1, source_target_pairs={{0,1},{1,2},{2,3},{4,5},{5,6},{6,7},{8,9},{9,10},{10,11},{12,13},{... | collective-permute-start | bytes 172040 | tf_op jit(solution)/shard_map/ppermute | solution.py:203
  69.7 0.0 collective-permute-done.1.hd_ref
  69.7 1.2 %collective-permute-done.hu_ref = f32[14,4,256]{2,1,0:T(4,128)S(1)} collective-permute-done((f32[14,4,256]{2,1,0:T(4,128)S(1)}, f32[14,4,256]{2,1,0:T(4,128)S(1)}, u32[]{:S(2)}, u32[]{:S(2)}) %collective-permute-start) | collective-permute-done | bytes 57376 | tf_op jit(solution)/shard_map/ppermute | solution.py:203
  71.0 8.1 %shard_map.92 = f32[14,14,32,256]{3,2,1,0:T(8,128)} custom-call(f32[14,14,32,256]{3,2,1,0:T(8,128)} %bitcast.26, f32[14,4,256]{2,1,0:T(4,128)S(1)} %collective-permute-done.hu_ref, f32[14,4,256]{2,1,0:T(4,128)S(1)} %collective-permute-done.1.hd_ref), custom_call_target="tpu_custom_call" | custom-call | flops 16056320 | bytes 12845056 | tf_op jit(solution)/shard_map/pallas_call | solution.py:164
  (1 shorter events, 0.0 us)
Async XLA Ops:
  62.6 7.1 %collective-permute-start.1 = (f32[14,4,256]{2,1,0:T(4,128)S(1)}, f32[14,4,256]{2,1,0:T(4,128)S(1)}, u32[]{:S(2)}, u32[]{:S(2)}) collective-permute-start(f32[14,4,256]{2,1,0:T(4,128)S(1)} %get-tuple-element.5), channel_id=1, source_target_pairs={{1,0},{2,1},{3,2},{5,4},{6,5},{7,6},{9,8},{10,9},{11,10},{13,12},{... | collective-permute-start | bytes 172040 | tf_op jit(solution)/shard_map/ppermute | solution.py:204
  64.6 6.4 %collective-permute-start = (f32[14,4,256]{2,1,0:T(4,128)S(1)}, f32[14,4,256]{2,1,0:T(4,128)S(1)}, u32[]{:S(2)}, u32[]{:S(2)}) collective-permute-start(f32[14,4,256]{2,1,0:T(4,128)S(1)} %get-tuple-element.6), channel_id=1, source_target_pairs={{0,1},{1,2},{2,3},{4,5},{5,6},{6,7},{8,9},{9,10},{10,11},{12,13},{... | collective-permute-start | bytes 172040 | tf_op jit(solution)/shard_map/ppermute | solution.py:203

commit v6 on v5

--- a/solution.py
+++ b/solution.py
@@ -178,6 +178,43 @@
     return out.reshape(cells, slots, emb)
 
 
+def row_box(halo):
+    before = jnp.concatenate(
+        [jnp.pad(halo[TILE - 1 :, :-1], ((0, 0), (1, 0), (0, 0))), halo[:-1]], axis=0
+    )
+    after = jnp.concatenate([halo[1:], jnp.pad(halo[:1, 1:], ((0, 0), (0, 1), (0, 0)))], axis=0)
+    return (before + halo + after) / 9.0
+
+
+def fix_kernel(a_ref, hu_ref, hd_ref, o_ref):
+    g = pl.program_id(0)
+    slots = a_ref.shape[2]
+    o_ref[...] = a_ref[...]
+
+    @pl.when(g == 0)
+    def _():
+        o_ref[0, :, 0:TCOLS, :] = a_ref[0, :, 0:TCOLS, :] + hu_ref[...]
+
+    @pl.when(g == 1)
+    def _():
+        o_ref[0, :, slots - TCOLS :, :] = a_ref[0, :, slots - TCOLS :, :] + hd_ref[...]
+
+
+def add_halo_rows(averaged, up, down):
+    cells, slots, emb = averaged.shape
+    a4 = averaged.reshape(TILE, TILE, slots, emb)
+    row = pl.BlockSpec((1, TILE, slots, emb), lambda g: (g * (TILE - 1), 0, 0, 0))
+    out = pl.pallas_call(
+        fix_kernel,
+        grid=(2,),
+        in_specs=[row, pl.BlockSpec(up.shape, lambda g: (0, 0, 0)), pl.BlockSpec(down.shape, lambda g: (0, 0, 0))],
+        out_specs=row,
+        out_shape=jax.ShapeDtypeStruct(a4.shape, jnp.float32),
+        input_output_aliases={0: 0},
+    )(a4, up, down)
+    return out.reshape(cells, slots, emb)
+
+
 def per_device(
     tiles, counts, tissue_mask, w_reduce, b_reduce, w_spatial, b_spatial, w_expand, proj_w
 ):
@@ -202,7 +239,9 @@
     backward = [(target, source) for source, target in forward]
     up = lax.ppermute(computed[CELLS - TILE :, slots - TCOLS :], "region", forward)
     down = lax.ppermute(computed[:TILE, :TCOLS], "region", backward)
-    averaged = grid_box_average(computed, up, down)
+    none = jnp.zeros(up.shape, up.dtype)
+    averaged = grid_box_average(computed, none, none)
+    averaged = add_halo_rows(averaged, row_box(up), row_box(down))
     return jnp.transpose(averaged, (1, 0, 2)).reshape(1, 1, slots, CELLS, -1)
 
 

time: 80.7 us -> 81.9 us (1.015)
  the two profiles are of different devices: /device:TPU:1 before, /device:TPU:39 now
where the time goes in v6:
time: 81.9 us; the launch traced here: 81.6 us
  Pallas kernels  67.8 us (83%)
  starting transfers between devices  7.3 us (9%)
  local copies, waits for them, and re-layouts  3.54 us (4%)
  other arithmetic  2.18 us (3%)
    pallas_call x1, Pallas kernels, cell_features(): pl.pallas_call(cell_kernel, grid_spec=grid_spec, out_shape=jax.ShapeDtype...  57.6 us
    pallas_call x1, Pallas kernels, grid_box_average(): pl.pallas_call(grid_box_kernel, out_shape=jax.ShapeDtypeStruct(w4.shape,...  8.13 us
    ppermute x1, starting transfers between devices, per_device(): lax.ppermute(computed[CELLS - TILE:, slots - TCOLS:], 'region', forward)  5.38 us
    convert_element_type x1, local copies, waits for them, and re-layouts, per_device(): weight.T[:, :, None].astype(jnp.bfloat16)  2.52 us
    pallas_call x1, Pallas kernels, add_halo_rows(): pl.pallas_call(fix_kernel, grid=(2,), in_specs=[row, pl.BlockSpec(up.shap...  2.02 us
    ppermute x1, starting transfers between devices, per_device(): down = lax.ppermute(computed[:TILE, :TCOLS], 'region', backward)  1.92 us
  transfers between devices with their start and end apart: 2, of which 0 were waited for; matrix products, arithmetic and copies ran while one was open for 0% of the time, Pallas kernels for 10%

profile of v6, /device:TPU:39, one launch (start us, length us, event | category | flops | bytes accessed | tf_op | source)
XLA Modules:
  0.0 81.6 jit_solution(7693865353045115709)
XLA Ops:
  0.7 0.8 %fusion.8 = bf16[196,32,1]{0,1,2:T(8,128)(2,1)S(1)} fusion(s32[1,1,32,196]{3,2,1,0:T(8,128)} %param.11, pred[32]{0:T(512)(128)(4,1)S(1)} %iota_compare_fusion.2), kind=kLoop, calls=%fused_computation.15 | loop fusion | flops 18816 | bytes 37664 | tf_op jit(solution)/shard_map/convert_element_type | solution.py:229
  1.5 2.5 %copy.12.m_ref = bf16[196,32,1]{2,1,0:T(8,128)(2,1)} copy(bf16[196,32,1]{0,1,2:T(8,128)(2,1)S(1)} %fusion.8) | data formatting | bytes 25088 | tf_op jit(solution)/shard_map/convert_element_type | solution.py:229
  4.0 57.6 %shard_map.91 = f32[196,32,256]{2,1,0:T(8,128)} custom-call(s32[1]{0:T(128)} %bitcast.24.count_ref, bf16[196,32,1024]{2,1,0:T(8,128)(2,1)} %bitcast.27, bf16[196,32,1]{2,1,0:T(8,128)(2,1)} %copy.12.m_ref, bf16[2,1024,256]{2,1,0:T(8,128)(2,1)} %wr_ref.1, f32[2,256]{1,0:T(2,128)} %br_ref.1, bf16[2,3,768,256]{3,2,1,0:T(8,128)(2,1)} %bitcast.28, ...), custom_call_target="tpu_custom_call" | custom-call | flops 31239176192 | bytes 19292672 | tf_op jit(solution)/shard_map/pallas_call | solution.py:117
  61.7 1.0 %fusion.9 = (f32[14,4,256]{2,1,0:T(4,128)S(1)}, f32[14,4,256]{2,1,0:T(4,128)S(1)}) fusion(f32[196,32,256]{2,1,0:T(8,128)} %shard_map.91), kind=kLoop, calls=%fused_computation.17 | loop fusion | bytes 229376 | tf_op jit(solution)/shard_map/slice | solution.py:241
  62.6 5.4 %collective-permute-start = (f32[14,4,256]{2,1,0:T(4,128)S(1)}, f32[14,4,256]{2,1,0:T(4,128)S(1)}, u32[]{:S(2)}, u32[]{:S(2)}) collective-permute-start(f32[14,4,256]{2,1,0:T(4,128)S(1)} %get-tuple-element.6), channel_id=1, source_target_pairs={{0,1},{1,2},{2,3},{4,5},{5,6},{6,7},{8,9},{9,10},{10,11},{12,13},{... | collective-permute-start | bytes 172040 | tf_op jit(solution)/shard_map/ppermute | solution.py:240
  68.0 1.9 %collective-permute-start.1 = (f32[14,4,256]{2,1,0:T(4,128)S(1)}, f32[14,4,256]{2,1,0:T(4,128)S(1)}, u32[]{:S(2)}, u32[]{:S(2)}) collective-permute-start(f32[14,4,256]{2,1,0:T(4,128)S(1)} %get-tuple-element.5), channel_id=1, source_target_pairs={{1,0},{2,1},{3,2},{5,4},{6,5},{7,6},{9,8},{10,9},{11,10},{13,12},{... | collective-permute-start | bytes 172040 | tf_op jit(solution)/shard_map/ppermute | solution.py:241
  70.0 8.1 %shard_map.92.a_ref = f32[14,14,32,256]{3,2,1,0:T(8,128)} custom-call(f32[14,14,32,256]{3,2,1,0:T(8,128)} %bitcast.26, f32[14,4,256]{2,1,0:T(4,128)S(1)} %broadcast_in_dim.19.hu_ref.hd_ref, f32[14,4,256]{2,1,0:T(4,128)S(1)} %broadcast_in_dim.19.hu_ref.hd_ref), custom_call_target="tpu_custom_call" | custom-call | flops 16056320 | bytes 12845056 | tf_op jit(solution)/shard_map/pallas_call | solution.py:164
  78.1 0.0 collective-permute-done
  78.1 0.0 collective-permute-done.1
  78.2 0.7 fusion.4.hu_ref
  78.9 0.7 fusion.1.hd_ref
  79.5 2.0 %shard_map.93 = f32[14,14,32,256]{3,2,1,0:T(8,128)} custom-call(f32[14,14,32,256]{3,2,1,0:T(8,128)} %shard_map.92.a_ref, f32[14,4,256]{2,1,0:T(4,128)} %fusion.4.hu_ref, f32[14,4,256]{2,1,0:T(4,128)} %fusion.1.hd_ref), custom_call_target="tpu_custom_call", output_to_operand_aliasing={{}: (0, {})} | custom-call | tf_op jit(solution)/shard_map/pallas_call | solution.py:207
  (6 shorter events, 0.1 us)
Async XLA Ops:
  62.6 15.5 %collective-permute-start = (f32[14,4,256]{2,1,0:T(4,128)S(1)}, f32[14,4,256]{2,1,0:T(4,128)S(1)}, u32[]{:S(2)}, u32[]{:S(2)}) collective-permute-start(f32[14,4,256]{2,1,0:T(4,128)S(1)} %get-tuple-element.6), channel_id=1, source_target_pairs={{0,1},{1,2},{2,3},{4,5},{5,6},{6,7},{8,9},{9,10},{10,11},{12,13},{... | collective-permute-start | bytes 172040 | tf_op jit(solution)/shard_map/ppermute | solution.py:240
  68.0 10.1 %collective-permute-start.1 = (f32[14,4,256]{2,1,0:T(4,128)S(1)}, f32[14,4,256]{2,1,0:T(4,128)S(1)}, u32[]{:S(2)}, u32[]{:S(2)}) collective-permute-start(f32[14,4,256]{2,1,0:T(4,128)S(1)} %get-tuple-element.5), channel_id=1, source_target_pairs={{1,0},{2,1},{3,2},{5,4},{6,5},{7,6},{9,8},{10,9},{11,10},{13,12},{... | collective-permute-start | bytes 172040 | tf_op jit(solution)/shard_map/ppermute | solution.py:241

commit v7 on v5

--- a/solution.py
+++ b/solution.py
@@ -22,16 +22,27 @@
 
 
 def cell_kernel(
-    count_ref, x_ref, m_ref, wr_ref, br_ref, ws_ref, bs_ref, we_ref, pw_ref, o_ref,
+    count_ref, x_ref, m_ref, wr_ref, br_ref, ws_ref, bs_ref, we_ref, pw_ref, o_ref, hu_ref, hd_ref,
     cur_ref, r_ref, c_ref,
 ):
     g = pl.program_id(0)
     total = CELLS * GROUP
     chunks = CELLS // SPAN
 
+    last = pl.num_programs(0) - 1
+    cells = o_ref.shape[0]
+
     @pl.when(g * GROUP >= count_ref[0])
     def _():
         o_ref[...] = jnp.zeros(o_ref.shape, o_ref.dtype)
+
+        @pl.when(g == last)
+        def _():
+            hu_ref[...] = jnp.zeros(hu_ref.shape, hu_ref.dtype)
+
+        @pl.when(g == 0)
+        def _():
+            hd_ref[...] = jnp.zeros(hd_ref.shape, hd_ref.dtype)
 
     @pl.when(g * GROUP < count_ref[0])
     def _():
@@ -81,6 +92,14 @@
             c0 = ch * SPAN
             o_ref[pl.ds(c0, SPAN)] = proj.reshape(SPAN, GROUP, -1) * m_ref[pl.ds(c0, SPAN)]
 
+        @pl.when(g == last)
+        def _():
+            hu_ref[...] = o_ref[cells - TILE :, GROUP - TCOLS :, :]
+
+        @pl.when(g == 0)
+        def _():
+            hd_ref[...] = o_ref[0:TILE, 0:TCOLS, :]
+
 
 def cell_features(count, xt, weight, w_reduce, b_reduce, w_spatial, b_spatial, w_expand, proj_w):
     cells, slots, _ = xt.shape
@@ -106,7 +125,11 @@
             pl.BlockSpec((BLOCKS, MID, CHAN), whole(3), pipeline_mode=once),
             pl.BlockSpec((CHAN, emb), whole(2), pipeline_mode=once),
         ],
-        out_specs=pl.BlockSpec((cells, GROUP, emb), lambda g, c: (0, g, 0)),
+        out_specs=[
+            pl.BlockSpec((cells, GROUP, emb), lambda g, c: (0, g, 0)),
+            pl.BlockSpec((TILE, TCOLS, emb), lambda g, c: (0, 0, 0)),
+            pl.BlockSpec((TILE, TCOLS, emb), lambda g, c: (0, 0, 0)),
+        ],
         scratch_shapes=[
             pltpu.VMEM((cells * GROUP, CHAN), jnp.bfloat16),
             pltpu.VMEM((cells * GROUP + 2 * GROUP, MID), jnp.float32),
@@ -117,7 +140,11 @@
     return pl.pallas_call(
         cell_kernel,
         grid_spec=grid_spec,
-        out_shape=jax.ShapeDtypeStruct((cells, slots, emb), jnp.float32),
+        out_shape=[
+            jax.ShapeDtypeStruct((cells, slots, emb), jnp.float32),
+            jax.ShapeDtypeStruct((TILE, TCOLS, emb), jnp.float32),
+            jax.ShapeDtypeStruct((TILE, TCOLS, emb), jnp.float32),
+        ],
         compiler_params=pltpu.CompilerParams(
             dimension_semantics=("arbitrary",), vmem_limit_bytes=60 * 1024 * 1024
         ),
@@ -186,7 +213,7 @@
     positions = jnp.arange(slots, dtype=jnp.int32)
     alive = positions < held[0]
     weight = jnp.where(alive[:, None], tissue_mask[0, 0], 0).astype(jnp.float32)
-    computed = cell_features(
+    computed, last_row, first_row = cell_features(
         held,
         jnp.transpose(tiles[0, 0], (1, 0, 2)),
         weight.T[:, :, None].astype(jnp.bfloat16),
@@ -200,8 +227,8 @@
     count = lax.axis_size("region")
     forward = [(i, i + 1) for i in range(count - 1)]
     backward = [(target, source) for source, target in forward]
-    up = lax.ppermute(computed[CELLS - TILE :, slots - TCOLS :], "region", forward)
-    down = lax.ppermute(computed[:TILE, :TCOLS], "region", backward)
+    up = lax.ppermute(last_row, "region", forward)
+    down = lax.ppermute(first_row, "region", backward)
     averaged = grid_box_average(computed, up, down)
     return jnp.transpose(averaged, (1, 0, 2)).reshape(1, 1, slots, CELLS, -1)
 

time: 80.7 us -> 83.5 us (1.035); the launches traced: 79.1 us -> 83.3 us
  starting transfers between devices: 7.07 us -> 32.9 us
  Pallas kernels: 65.8 us -> 41 us
  waiting for transfers between devices: 1.23 us -> 5.28 us
  local copies, waits for them, and re-layouts: 3.49 us -> 2.52 us
    ppermute x2, starting transfers between devices: 7.07 us -> 32.9 us  [the longest x1 31 us: per_device(): up = lax.ppermute(last_row, 'region', forward)]
    pallas_call x1, Pallas kernels: 57.7 us -> 32.9 us  [cell_features(): pl.pallas_call(cell_kernel, grid_spec=grid_spec, out_shape=[jax.ShapeDtyp...]
    ppermute x2, waiting for transfers between devices: 1.23 us -> 5.28 us  [the longest x1 5.27 us: per_device(): down = lax.ppermute(first_row, 'region', backward)]
    slice x1 -> x0, local copies, waits for them, and re-layouts: 0.98 us -> none  [per_device(): down = lax.ppermute(computed[:TILE, :TCOLS], 'region', backward)]
where the time goes in v7:
time: 83.5 us; the launch traced here: 83.3 us
  Pallas kernels  41 us (49%)
  starting transfers between devices  32.9 us (39%)
  waiting for transfers between devices  5.28 us (6%)
  local copies, waits for them, and re-layouts  2.52 us (3%)
  other arithmetic  0.84 us (1%)
    pallas_call x1, Pallas kernels, cell_features(): pl.pallas_call(cell_kernel, grid_spec=grid_spec, out_shape=[jax.ShapeDtyp...  32.9 us
    ppermute x1, starting transfers between devices, per_device(): up = lax.ppermute(last_row, 'region', forward)  31 us
    pallas_call x1, Pallas kernels, grid_box_average(): pl.pallas_call(grid_box_kernel, out_shape=jax.ShapeDtypeStruct(w4.shape,...  8.13 us
    ppermute x1, waiting for transfers between devices, per_device(): down = lax.ppermute(first_row, 'region', backward)  5.27 us
    convert_element_type x1, local copies, waits for them, and re-layouts, per_device(): weight.T[:, :, None].astype(jnp.bfloat16)  2.52 us
    ppermute x1, starting transfers between devices, per_device(): down = lax.ppermute(first_row, 'region', backward)  1.92 us
  transfers between devices with their start and end apart: 2, of which 1 were waited for; matrix products, arithmetic and copies ran while one was open for 0% of the time, Pallas kernels for 0%

profile of v7, /device:TPU:1, one launch (start us, length us, event | category | flops | bytes accessed | tf_op | source)
XLA Modules:
  0.0 83.3 jit_solution(12996694819041570196)
XLA Ops:
  0.7 0.8 %fusion.2 = bf16[196,32,1]{0,1,2:T(8,128)(2,1)S(1)} fusion(s32[1,1,32,196]{3,2,1,0:T(8,128)} %param.11, pred[32]{0:T(512)(128)(4,1)S(1)} %iota_compare_fusion), kind=kLoop, calls=%fused_computation.3 | loop fusion | flops 18816 | bytes 37664 | tf_op jit(solution)/shard_map/convert_element_type | solution.py:219
  1.5 2.5 %copy.11.m_ref = bf16[196,32,1]{2,1,0:T(8,128)(2,1)} copy(bf16[196,32,1]{0,1,2:T(8,128)(2,1)S(1)} %fusion.2) | data formatting | bytes 25088 | tf_op jit(solution)/shard_map/convert_element_type | solution.py:219
  4.0 32.9 %shard_map.91 = (f32[196,32,256]{2,1,0:T(8,128)}, f32[14,4,256]{2,1,0:T(4,128)}, f32[14,4,256]{2,1,0:T(4,128)}) custom-call(s32[1]{0:T(128)} %bitcast.24.count_ref, bf16[196,32,1024]{2,1,0:T(8,128)(2,1)} %bitcast.27, bf16[196,32,1]{2,1,0:T(8,128)(2,1)} %copy.11.m_ref, bf16[2,1024,256]{2,1,0:T(8,128)(2,1)} %wr_ref.1, f32[2,256]{1,0:T(2,128)} %br_ref.1, ...), custom_call_target="tpu_custom_call" | custom-call | flops 31239176192 | bytes 19292672 | tf_op jit(solution)/shard_map/pallas_call | solution.py:140
  36.9 31.0 %collective-permute-start = (f32[14,4,256]{2,1,0:T(4,128)}, f32[14,4,256]{2,1,0:T(4,128)S(1)}, u32[]{:S(2)}, u32[]{:S(2)}) collective-permute-start(f32[14,4,256]{2,1,0:T(4,128)} %get-tuple-element.9), channel_id=1, source_target_pairs={{0,1},{1,2},{2,3},{4,5},{5,6},{6,7},{8,9},{9,10},{10,11},{12,13},{... | collective-permute-start | bytes 172040 | tf_op jit(solution)/shard_map/ppermute | solution.py:230
  67.9 1.9 %collective-permute-start.1 = (f32[14,4,256]{2,1,0:T(4,128)}, f32[14,4,256]{2,1,0:T(4,128)S(1)}, u32[]{:S(2)}, u32[]{:S(2)}) collective-permute-start(f32[14,4,256]{2,1,0:T(4,128)} %get-tuple-element.10), channel_id=1, source_target_pairs={{1,0},{2,1},{3,2},{5,4},{6,5},{7,6},{9,8},{10,9},{11,10},{13,12},{... | collective-permute-start | bytes 172040 | tf_op jit(solution)/shard_map/ppermute | solution.py:231
  69.9 0.0 collective-permute-done.hu_ref
  69.9 5.3 %collective-permute-done.1.hd_ref = f32[14,4,256]{2,1,0:T(4,128)S(1)} collective-permute-done((f32[14,4,256]{2,1,0:T(4,128)}, f32[14,4,256]{2,1,0:T(4,128)S(1)}, u32[]{:S(2)}, u32[]{:S(2)}) %collective-permute-start.1) | collective-permute-done | bytes 57376 | tf_op jit(solution)/shard_map/ppermute | solution.py:231
  75.1 8.1 %shard_map.92 = f32[14,14,32,256]{3,2,1,0:T(8,128)} custom-call(f32[14,14,32,256]{3,2,1,0:T(8,128)} %bitcast.26, f32[14,4,256]{2,1,0:T(4,128)S(1)} %collective-permute-done.hu_ref, f32[14,4,256]{2,1,0:T(4,128)S(1)} %collective-permute-done.1.hd_ref), custom_call_target="tpu_custom_call" | custom-call | flops 16056320 | bytes 12845056 | tf_op jit(solution)/shard_map/pallas_call | solution.py:191
  (1 shorter events, 0.0 us)
Async XLA Ops:
  36.9 33.0 %collective-permute-start = (f32[14,4,256]{2,1,0:T(4,128)}, f32[14,4,256]{2,1,0:T(4,128)S(1)}, u32[]{:S(2)}, u32[]{:S(2)}) collective-permute-start(f32[14,4,256]{2,1,0:T(4,128)} %get-tuple-element.9), channel_id=1, source_target_pairs={{0,1},{1,2},{2,3},{4,5},{5,6},{6,7},{8,9},{9,10},{10,11},{12,13},{... | collective-permute-start | bytes 172040 | tf_op jit(solution)/shard_map/ppermute | solution.py:230
  67.9 7.2 %collective-permute-start.1 = (f32[14,4,256]{2,1,0:T(4,128)}, f32[14,4,256]{2,1,0:T(4,128)S(1)}, u32[]{:S(2)}, u32[]{:S(2)}) collective-permute-start(f32[14,4,256]{2,1,0:T(4,128)} %get-tuple-element.10), channel_id=1, source_target_pairs={{1,0},{2,1},{3,2},{5,4},{6,5},{7,6},{9,8},{10,9},{11,10},{13,12},{... | collective-permute-start | bytes 172040 | tf_op jit(solution)/shard_map/ppermute | solution.py:231

commit v8 on v5

--- a/solution.py
+++ b/solution.py
@@ -79,7 +79,7 @@
             q0 = ch * ROWS
             proj = jnp.dot(cur_ref[pl.ds(q0, ROWS), :], pw_ref[...], preferred_element_type=jnp.float32)
             c0 = ch * SPAN
-            o_ref[pl.ds(c0, SPAN)] = proj.reshape(SPAN, GROUP, -1) * m_ref[pl.ds(c0, SPAN)]
+            o_ref[pl.ds(c0, SPAN)] = proj.reshape(SPAN, GROUP, -1) * m_ref[pl.ds(c0, SPAN)].astype(jnp.float32)
 
 
 def cell_features(count, xt, weight, w_reduce, b_reduce, w_spatial, b_spatial, w_expand, proj_w):
@@ -189,7 +189,7 @@
     computed = cell_features(
         held,
         jnp.transpose(tiles[0, 0], (1, 0, 2)),
-        weight.T[:, :, None].astype(jnp.bfloat16),
+        weight.T[:, :, None].astype(jnp.int8),
         w_reduce,
         b_reduce,
         w_spatial,

time: 80.7 us -> 80.9 us (level); the launches traced: 79.1 us -> 80.4 us
  starting transfers between devices: 7.07 us -> 32.9 us
  Pallas kernels: 65.8 us -> 40.9 us
    pallas_call x1, Pallas kernels: 57.7 us -> 32.7 us  [cell_features(): pl.pallas_call(cell_kernel, grid_spec=grid_spec, out_shape=jax.ShapeDtype...]
    ppermute x1, starting transfers between devices: 5.15 us -> 29.6 us  [per_device(): lax.ppermute(computed[CELLS - TILE:, slots - TCOLS:], 'region', forward)]
    ppermute x1, starting transfers between devices: 1.92 us -> 3.29 us  [per_device(): down = lax.ppermute(computed[:TILE, :TCOLS], 'region', backward)]
where the time goes in v8:
time: 80.9 us; the launch traced here: 80.4 us
  Pallas kernels  40.9 us (51%)
  starting transfers between devices  32.9 us (41%)
  local copies, waits for them, and re-layouts  3.83 us (5%)
  waiting for transfers between devices  1.23 us (2%)
  other arithmetic  0.85 us (1%)
    pallas_call x1, Pallas kernels, cell_features(): pl.pallas_call(cell_kernel, grid_spec=grid_spec, out_shape=jax.ShapeDtype...  32.7 us
    ppermute x1, starting transfers between devices, per_device(): lax.ppermute(computed[CELLS - TILE:, slots - TCOLS:], 'region', forward)  29.6 us
    pallas_call x1, Pallas kernels, grid_box_average(): pl.pallas_call(grid_box_kernel, out_shape=jax.ShapeDtypeStruct(w4.shape,...  8.13 us
    ppermute x1, starting transfers between devices, per_device(): down = lax.ppermute(computed[:TILE, :TCOLS], 'region', backward)  3.29 us
    convert_element_type x1, local copies, waits for them, and re-layouts, per_device(): weight.T[:, :, None].astype(jnp.int8)  2.85 us
  transfers between devices with their start and end apart: 2, of which 1 were waited for; matrix products, arithmetic and copies ran while one was open for 0% of the time, Pallas kernels for 0%

profile of v8, /device:TPU:1, one launch (start us, length us, event | category | flops | bytes accessed | tf_op | source)
XLA Modules:
  0.0 80.4 jit_solution(9676975841511217225)
XLA Ops:
  0.7 0.8 %fusion.2 = s8[196,32,1]{0,1,2:T(8,128)(4,1)S(1)} fusion(s32[1,1,32,196]{3,2,1,0:T(8,128)} %param.11, pred[32]{0:T(512)(128)(4,1)S(1)} %iota_compare_fusion), kind=kLoop, calls=%fused_computation.3 | loop fusion | flops 18816 | bytes 31392 | tf_op jit(solution)/shard_map/convert_element_type | solution.py:192
  1.5 2.9 %copy.11.m_ref = s8[196,32,1]{2,1,0:T(8,128)(4,1)} copy(s8[196,32,1]{0,1,2:T(8,128)(4,1)S(1)} %fusion.2) | data formatting | bytes 12544 | tf_op jit(solution)/shard_map/convert_element_type | solution.py:192
  4.4 32.7 %shard_map.91 = f32[196,32,256]{2,1,0:T(8,128)} custom-call(s32[1]{0:T(128)} %bitcast.24.count_ref, bf16[196,32,1024]{2,1,0:T(8,128)(2,1)} %bitcast.27, s8[196,32,1]{2,1,0:T(8,128)(4,1)} %copy.11.m_ref, bf16[2,1024,256]{2,1,0:T(8,128)(2,1)} %wr_ref.1, f32[2,256]{1,0:T(2,128)} %br_ref.1, bf16[2,3,768,256]{3,2,1,0:T(8,128)(2,1)} %bitcast.28, f32[2,256]{1,0:T(2,128)} %bs_ref.1, ...), custom_call_target="tpu_custom_call" | custom-call | flops 31239176192 | bytes 19292672 | tf_op jit(solution)/shard_map/pallas_call | solution.py:117
  37.1 1.0 %fusion.3 = (f32[14,4,256]{2,1,0:T(4,128)S(1)}, f32[14,4,256]{2,1,0:T(4,128)S(1)}) fusion(f32[196,32,256]{2,1,0:T(8,128)} %shard_map.91), kind=kLoop, calls=%fused_computation.5 | loop fusion | bytes 229376 | tf_op jit(solution)/shard_map/slice | solution.py:204
  38.1 3.3 %collective-permute-start.1 = (f32[14,4,256]{2,1,0:T(4,128)S(1)}, f32[14,4,256]{2,1,0:T(4,128)S(1)}, u32[]{:S(2)}, u32[]{:S(2)}) collective-permute-start(f32[14,4,256]{2,1,0:T(4,128)S(1)} %get-tuple-element.5), channel_id=1, source_target_pairs={{1,0},{2,1},{3,2},{5,4},{6,5},{7,6},{9,8},{10,9},{11,10},{13,12},{... | collective-permute-start | bytes 172040 | tf_op jit(solution)/shard_map/ppermute | solution.py:204
  41.4 29.6 %collective-permute-start = (f32[14,4,256]{2,1,0:T(4,128)S(1)}, f32[14,4,256]{2,1,0:T(4,128)S(1)}, u32[]{:S(2)}, u32[]{:S(2)}) collective-permute-start(f32[14,4,256]{2,1,0:T(4,128)S(1)} %get-tuple-element.6), channel_id=1, source_target_pairs={{0,1},{1,2},{2,3},{4,5},{5,6},{6,7},{8,9},{9,10},{10,11},{12,13},{... | collective-permute-start | bytes 172040 | tf_op jit(solution)/shard_map/ppermute | solution.py:203
  71.0 0.0 collective-permute-done.1.hd_ref
  71.0 1.2 %collective-permute-done.hu_ref = f32[14,4,256]{2,1,0:T(4,128)S(1)} collective-permute-done((f32[14,4,256]{2,1,0:T(4,128)S(1)}, f32[14,4,256]{2,1,0:T(4,128)S(1)}, u32[]{:S(2)}, u32[]{:S(2)}) %collective-permute-start) | collective-permute-done | bytes 57376 | tf_op jit(solution)/shard_map/ppermute | solution.py:203
  72.3 8.1 %shard_map.92 = f32[14,14,32,256]{3,2,1,0:T(8,128)} custom-call(f32[14,14,32,256]{3,2,1,0:T(8,128)} %bitcast.26, f32[14,4,256]{2,1,0:T(4,128)S(1)} %collective-permute-done.hu_ref, f32[14,4,256]{2,1,0:T(4,128)S(1)} %collective-permute-done.1.hd_ref), custom_call_target="tpu_custom_call" | custom-call | flops 16056320 | bytes 12845056 | tf_op jit(solution)/shard_map/pallas_call | solution.py:164
  (1 shorter events, 0.0 us)
Async XLA Ops:
  38.1 33.0 %collective-permute-start.1 = (f32[14,4,256]{2,1,0:T(4,128)S(1)}, f32[14,4,256]{2,1,0:T(4,128)S(1)}, u32[]{:S(2)}, u32[]{:S(2)}) collective-permute-start(f32[14,4,256]{2,1,0:T(4,128)S(1)} %get-tuple-element.5), channel_id=1, source_target_pairs={{1,0},{2,1},{3,2},{5,4},{6,5},{7,6},{9,8},{10,9},{11,10},{13,12},{... | collective-permute-start | bytes 172040 | tf_op jit(solution)/shard_map/ppermute | solution.py:204
  41.4 30.9 %collective-permute-start = (f32[14,4,256]{2,1,0:T(4,128)S(1)}, f32[14,4,256]{2,1,0:T(4,128)S(1)}, u32[]{:S(2)}, u32[]{:S(2)}) collective-permute-start(f32[14,4,256]{2,1,0:T(4,128)S(1)} %get-tuple-element.6), channel_id=1, source_target_pairs={{0,1},{1,2},{2,3},{4,5},{5,6},{6,7},{8,9},{9,10},{10,11},{12,13},{... | collective-permute-start | bytes 172040 | tf_op jit(solution)/shard_map/ppermute | solution.py:203
